TPU v7x, 256 devices: a whole 4x4x8 slice. The times are simulated.
256 devices in a mesh: patch: 128 (over x, z, y), strip: 2 (over core).
Axes of the slice: x: 4, y: 4, z: 8, core: 2. Of those that a mesh axis runs over, the one named last changes fastest.
Arguments:
- features: float32 [262144, 128], P(('patch', 'strip')), may hold values from -6 to 6
- lap_tiles: float32 [4096, 6, 4096], P(('patch', 'strip')), may hold values from -0.3125 to 0.3125
- columns: int32 [4096, 6], P(('patch', 'strip')), may hold values from 0 to 4095, as said below
- weights: float32 [3, 64, 64], replicated, may hold values from -0.75 to 0.75
- bias_term: float32 [64], replicated, may hold values from -4 to 4
- cotangent: float32 [262144, 128], P(('patch', 'strip')), may hold values from -6 to 6
Outputs:
- output: float32 [262144, 128], P(('patch', 'strip'))
- input_grad: float32 [262144, 128], P(('patch', 'strip'))
- weight_grad: float32 [3, 64, 64], replicated
- bias_grad: float32 [64], replicated
Inputs may be any that keep to these rules, and one draw needn't show every extreme that they name: `columns`: entry 0 of a block's 6 entries is the block itself and entry 1 lies exactly 4 blocks before or after it; all entries of a block are distinct blocks within 4 of it in the cyclic order of the 4096 blocks.
All inputs are finite; a program needn't handle non-finite values.
Results may differ from a plain program's by a relative error of at most 0.0001.
Values sent between devices are 32-bit elements; how exact they have to be, the bound alone decides.
No kernel may reach another device: no remote copies, remote signals or barrier semaphores. Data moves between devices by JAX's collectives and lax.ppermute only.
A program may use at most 64 MiB of HBM per device.

v0:
```python
import math

import jax
import jax.numpy as jnp
from jax import lax
from jax.experimental import pallas as pl
from jax.experimental.pallas import tpu as pltpu
from jax.sharding import Mesh
from jax.sharding import PartitionSpec as P


C = 64
BATCH = 2
PB = 64
NB = 6
HB = 4
BLK_DEV = 16
ROWS = BLK_DEV * PB
RIM = HB * PB
EXT = BLK_DEV + 2 * HB
MID = BLK_DEV - 2 * HB
HALF = 3 * C // 4
W2 = BATCH * C
CHUNKS = PB * PB // 128
AXES = ("patch_0", "patch_1", "patch_2", "strip")
SHAPE = (4, 8, 4, 2)
BLOCKS = 4096
F32 = jnp.float32
BF16 = jnp.bfloat16
VMEM = pl.BlockSpec(memory_space=pltpu.VMEM)
SMEM = pl.BlockSpec(memory_space=pltpu.SMEM)
HBM = pl.BlockSpec(memory_space=pltpu.HBM)


def split(value):
    high = value.astype(BF16)
    return high, (value - high.astype(F32)).astype(BF16)


def mm(a, b):
    return jnp.dot(a, b, preferred_element_type=F32)


def mm_tn(a, b):
    return lax.dot_general(a, b, (((0,), (0,)), ((), ())), preferred_element_type=F32)


def slot_of(cols, b, j):
    return jnp.bitwise_and(cols[j, b] - cols[0, 0] + HB, BLOCKS - 1)


def is_first_core(cols):
    return jnp.bitwise_and(cols[0, 0] // BLK_DEV, 1) == 0


def rim_rows(cols):
    first = is_first_core(cols)
    low, high = 0, (BLK_DEV + HB) * PB
    return (
        pl.multiple_of(jnp.where(first, high, low), RIM),
        pl.multiple_of(jnp.where(first, low, high), RIM),
    )


def rim_half(row):
    return pl.multiple_of(jnp.where(row == 0, 0, RIM), RIM)


def rim_block(i):
    return jnp.where(i < HB, i, i + MID)


def mid_block(i):
    return i + HB


def block_rows(ref, i):
    return jnp.concatenate(
        [ref[pl.ds(i * PB, PB // 2, stride=2), :], ref[pl.ds(i * PB + 1, PB // 2, stride=2), :]],
        axis=0,
    )


def rows_of(slot):
    return pl.ds(pl.multiple_of(slot * PB, PB), PB)


def spread(cols, at_ref, vec_ref, acc, block):
    def one(i, carry):
        b = block(i)
        high, low = split(block_rows(vec_ref, i))
        rhs = jnp.concatenate([high, high, low, low], axis=0)
        at = at_ref[i]
        out = mm(jnp.concatenate([at, at], axis=1), rhs)
        for j in range(NB):
            rows = rows_of(slot_of(cols, b, j))
            acc[rows, :] = acc[rows, :] + out[j * PB : (j + 1) * PB]
        return carry

    lax.fori_loop(0, MID, one, 0, unroll=8)


def hop(cols, fa_ref, cat, out_ref, block):
    def one(i, carry):
        b = block(i)
        rhs = jnp.concatenate([cat[rows_of(slot_of(cols, b, j)), :] for j in range(NB)], axis=0)
        out = mm(fa_ref[i], rhs)
        out = out[:, :W2] + out[:, W2:]
        out = out[:PB] + out[PB:]
        out_ref[pl.ds(i * PB, PB // 2, stride=2), :] = out[: PB // 2]
        out_ref[pl.ds(i * PB + 1, PB // 2, stride=2), :] = out[PB // 2 :]
        return carry

    lax.fori_loop(0, MID, one, 0, unroll=8)


def put_cat(cat, start, value):
    high, low = split(value)
    cat[pl.ds(start, value.shape[0]), :] = jnp.concatenate([high, low], axis=1)


def build(raw, fa_ref, at_ref, block, start=0, stop=MID):
    low_lanes = lax.broadcasted_iota(jnp.int32, (CHUNKS, 128), 1) < PB

    def one(i, carry):
        b = block(i)
        group, rows = b // 8, pl.ds(b % 8, CHUNKS, stride=8)
        for pair in range(NB // 2):
            even = raw[2 * pair, group, rows, :]
            odd = raw[2 * pair + 1, group, rows, :]
            top = jnp.where(low_lanes, even, pltpu.roll(odd, PB, 1))
            bottom = jnp.where(low_lanes, pltpu.roll(even, PB, 1), odd)
            both = jnp.concatenate([top, bottom], axis=0)
            high = both.astype(BF16)
            low = (both - high.astype(F32)).astype(BF16)
            lanes = pl.ds(pair * 128, 128)
            stacked = jnp.concatenate([high, low], axis=0)
            fa_ref[i, :, lanes] = stacked
            at_ref[i, lanes, :] = stacked.T
        return carry

    lax.fori_loop(start, stop, one, 0, unroll=4)


def rim_kernel(
    cols_hbm, tiles, g_hbm, x_hbm,
    cols_ref, raw, fa_ref, at_ref, acc, send_a, send_b,
    cols, g_rim, x_rim, sem, small,
):
    to_cols = pltpu.make_async_copy(cols_hbm, cols, small.at[0])
    others = [pltpu.make_async_copy(cols_hbm, cols_ref, small.at[1])]
    for n, (value, to) in enumerate(((g_hbm, g_rim), (x_hbm, x_rim))):
        others.append(
            pltpu.make_async_copy(value.at[pl.ds(0, RIM)], to.at[pl.ds(0, RIM)], small.at[2 + 2 * n])
        )
        others.append(
            pltpu.make_async_copy(
                value.at[pl.ds(ROWS - RIM, RIM)], to.at[pl.ds(RIM, RIM)], small.at[3 + 2 * n]
            )
        )
    copies = [
        pltpu.make_async_copy(
            tiles.at[:, pl.ds(8 * group, 8), pl.ds(k * 128, 128)],
            raw.at[:, group, pl.ds(8 * k, 8), :],
            sem.at[group * CHUNKS + k],
        )
        for group in range(BLK_DEV // 8)
        for k in range(CHUNKS)
    ]
    for copy in copies + [to_cols] + others:
        copy.start()
    acc[...] = jnp.zeros_like(acc)
    for copy in copies[:CHUNKS]:
        copy.wait()
    build(raw, fa_ref, at_ref, rim_block, 0, HB)
    for copy in copies[CHUNKS:]:
        copy.wait()
    build(raw, fa_ref, at_ref, rim_block, HB, MID)
    to_cols.wait()
    for copy in others:
        copy.wait()
    spread(cols, at_ref, g_rim, acc, rim_block)
    for row, send in zip(rim_rows(cols), (send_a, send_b)):
        send[0:RIM, :] = x_rim[pl.ds(rim_half(row), RIM), :]
        send[RIM : 2 * RIM, :] = acc[pl.ds(row, RIM), :]


def maps_sum(full):
    return full[:C] + pltpu.roll(full[C:], C, 1)


def products(left, right):
    a = jnp.concatenate([h for value in left for h in split(value)], axis=1)
    b = jnp.concatenate([h for value in right for h in split(value)], axis=1)
    out = mm_tn(a, b)
    result = []
    for p in range(len(left)):
        band = out[2 * p * W2 : (2 * p + 1) * W2] + out[(2 * p + 1) * W2 : (2 * p + 2) * W2]
        result.append(
            [
                band[:, 2 * q * W2 : (2 * q + 1) * W2] + band[:, (2 * q + 1) * W2 : (2 * q + 2) * W2]
                for q in range(len(right))
            ]
        )
    return result


def packed(zero, one, two):
    low_lanes = lax.broadcasted_iota(jnp.int32, (C, 128), 1) < C
    two = maps_sum(two)
    one = pltpu.roll(maps_sum(one), C, 1)
    if zero is None:
        top = jnp.where(low_lanes, 0.0, one)
    else:
        top = jnp.where(low_lanes, maps_sum(zero), one)
    bottom = jnp.where(low_lanes[: C // 2], two[: C // 2], pltpu.roll(two[C // 2 :], C, 1))
    return jnp.concatenate([top, bottom], axis=0)


def both_maps(weight):
    zero = jnp.zeros_like(weight)
    return jnp.concatenate(
        [jnp.concatenate([weight, zero], axis=1), jnp.concatenate([zero, weight], axis=1)], axis=0
    )


def mixed(value, weight):
    high, low = split(value)
    w_high, w_low = split(weight)
    row = jnp.concatenate([w_high, w_low], axis=1)
    out = mm(jnp.concatenate([high, low], axis=1), jnp.concatenate([row, row], axis=0))
    return out[:, :W2] + out[:, W2:]


def mid_kernel(
    cols, raw, g_ref, x_ref, acc_in,
    fa_ref, at_ref, first_ref, u_mid, u_rim, part_ref, cat,
    acc, *, scale,
):
    put_cat(cat, RIM, x_ref[...])
    acc[...] = acc_in[...]
    build(raw, fa_ref, at_ref, mid_block)
    g_mid = g_ref.at[pl.ds(RIM, MID * PB)]
    spread(cols, at_ref, g_mid, acc, mid_block)
    u_mid[...] = acc[2 * RIM : 4 * RIM, :]
    u_rim[0:RIM, :] = acc[RIM : 2 * RIM, :]
    u_rim[RIM : 2 * RIM, :] = acc[4 * RIM : 5 * RIM, :]
    hop(cols, fa_ref, cat, first_ref, mid_block)
    ((zero,),) = products([x_ref[...]], [g_ref[...]])
    ((one, two),) = products([first_ref[...]], [g_mid[...], u_mid[...]])
    part_ref[0 : C + C // 2, :] = scale * packed(zero, one, 2.0 * two - zero)
    bias = scale * jnp.sum(g_ref[...], axis=0, keepdims=True)
    part_ref[C + C // 2 :, :] = jnp.broadcast_to(bias + pltpu.roll(bias, C, 1), (8, 128))


def meet_kernel(
    cols, fa_ref, cat_in, r_a, r_b, g_ref, u_part, part_ref,
    first_ref, u_ref, keep_ref, give_ref, cat, *, scale
):
    del cat_in
    for row, r in zip(rim_rows(cols), (r_a, r_b)):
        put_cat(cat, row, r[0:RIM, :])
        half = pl.ds(rim_half(row), RIM)
        u_ref[half, :] = u_part[half, :] + r[RIM : 2 * RIM, :]
    hop(cols, fa_ref, cat, first_ref, rim_block)
    g_rim = jnp.concatenate([g_ref[0:RIM, :], g_ref[ROWS - RIM :, :]], axis=0)
    ((one, two),) = products([first_ref[...]], [g_rim, u_ref[...]])
    total = part_ref[0 : 2 * HALF, :] + scale * packed(None, one, 2.0 * two)
    first = is_first_core(cols)
    keep_ref[0:HALF, :] = jnp.where(first, total[:HALF], total[HALF:])
    give_ref[0:HALF, :] = jnp.where(first, total[HALF:], total[:HALF])
    keep_ref[HALF:, :] = part_ref[2 * HALF :, :]
    give_ref[HALF:, :] = part_ref[2 * HALF :, :]


def inner_rows(g, u, w_ref):
    return mixed(g, both_maps(w_ref[1]).T) + 2.0 * mixed(u, both_maps(w_ref[2]).T)


def inner_mid_kernel(cols, at_ref, g_ref, u_ref, w_ref, acc, inner):
    inner[...] = inner_rows(g_ref[RIM : ROWS - RIM, :], u_ref[...], w_ref)
    acc[...] = jnp.zeros_like(acc)
    spread(cols, at_ref, inner, acc, mid_block)


def inner_rim_kernel(
    cols, at_ref, g_ref, u_ref, w_ref, first_ref, acc_in, u2_ref, send_a, send_b, inner, acc
):
    g_rim = jnp.concatenate([g_ref[0:RIM, :], g_ref[ROWS - RIM :, :]], axis=0)
    inner[...] = inner_rows(g_rim, u_ref[...], w_ref)
    acc[...] = acc_in[...]
    spread(cols, at_ref, inner, acc, rim_block)
    u2_ref[...] = acc[RIM : RIM + ROWS, :]
    for row, send in zip(rim_rows(cols), (send_a, send_b)):
        send[0:RIM, :] = first_ref[pl.ds(rim_half(row), RIM), :]
        send[RIM : 2 * RIM, :] = acc[pl.ds(row, RIM), :]


def outputs(x, g, one, hopped, w_ref, bias_ref):
    bias = bias_ref[...]
    out = (
        mixed(x, both_maps(w_ref[0]))
        + mixed(one, both_maps(w_ref[1]))
        + mixed(2.0 * hopped - x, both_maps(w_ref[2]))
        + jnp.concatenate([bias, bias], axis=1)
    )
    return out, mixed(g, both_maps(w_ref[0] - w_ref[2]).T)


def own_cat(cat, f_mid, f_rim):
    put_cat(cat, RIM, f_rim[0:RIM, :])
    put_cat(cat, 2 * RIM, f_mid[...])
    put_cat(cat, 4 * RIM, f_rim[RIM : 2 * RIM, :])


def last_mid_kernel(
    cols, fa_ref, x_ref, g_ref, f_mid, f_rim, u2_ref, w_ref, bias_ref,
    out_hbm, back_hbm, cat, second, out_ref, back_ref, sem,
):
    own_cat(cat, f_mid, f_rim)
    hop(cols, fa_ref, cat, second, mid_block)
    mid = slice(RIM, ROWS - RIM)
    out, back = outputs(x_ref[mid, :], g_ref[mid, :], f_mid[...], second[...], w_ref, bias_ref)
    out_ref[...] = out
    back_ref[...] = back + u2_ref[mid, :]
    copies = [
        pltpu.make_async_copy(value, to.at[pl.ds(RIM, MID * PB)], sem.at[n])
        for n, (value, to) in enumerate(((out_ref, out_hbm), (back_ref, back_hbm)))
    ]
    for copy in copies:
        copy.start()
    for copy in copies:
        copy.wait()


def last_rim_kernel(
    cols, fa_ref, x_ref, g_ref, f_mid, f_rim, r_a, r_b, u2_ref, w_ref, bias_ref, o_in, b_in,
    out_hbm, back_hbm, cat, second, out_ref, back_ref, sem,
):
    del o_in, b_in
    own_cat(cat, f_mid, f_rim)
    for row, r in zip(rim_rows(cols), (r_a, r_b)):
        put_cat(cat, row, r[0:RIM, :])
    hop(cols, fa_ref, cat, second, rim_block)
    x = jnp.concatenate([x_ref[0:RIM, :], x_ref[ROWS - RIM :, :]], axis=0)
    g = jnp.concatenate([g_ref[0:RIM, :], g_ref[ROWS - RIM :, :]], axis=0)
    out, back = outputs(x, g, f_rim[...], second[...], w_ref, bias_ref)
    out_ref[...] = out
    back_ref[...] = back + jnp.concatenate([u2_ref[0:RIM, :], u2_ref[ROWS - RIM :, :]], axis=0)
    for row, r in zip(rim_rows(cols), (r_a, r_b)):
        half = pl.ds(rim_half(row), RIM)
        back_ref[half, :] = back_ref[half, :] + r[RIM : 2 * RIM, :]
    copies = [
        pltpu.make_async_copy(
            value.at[pl.ds(n * RIM, RIM)], to.at[pl.ds(n * (ROWS - RIM), RIM)], sem.at[2 * k + n]
        )
        for k, (value, to) in enumerate(((out_ref, out_hbm), (back_ref, back_hbm)))
        for n in range(2)
    ]
    for copy in copies:
        copy.start()
    for copy in copies:
        copy.wait()


def pairs_kernel(cols, own, near, following, far, total_ref):
    place = cols[0:1, 0:1] // BLK_DEV
    z = jnp.bitwise_and(place // 8, 7)
    q, step = z // 2, 2 * jnp.bitwise_and(z, 1) - 1
    at = [jnp.bitwise_and(q + offset, 3) for offset in (0, step, -step)]
    terms = []
    for k in range(4):
        term = far[...]
        for source, value in zip(at, (own, near, following)):
            term = jnp.where(jnp.broadcast_to(source, term.shape) == k, value[...], term)
        terms.append(term)
    total_ref[...] = (terms[0] + terms[1]) + (terms[2] + terms[3])


def final_kernel(cols, mine, theirs, weight_ref, bias_ref):
    core = jnp.bitwise_and(cols[0:1, 0:1] // BLK_DEV, 1)
    first = jnp.broadcast_to(core, mine.shape) == 0
    top = jnp.where(first, mine[...], theirs[...])
    bottom = jnp.where(first, theirs[...], mine[...])
    rest = C - HALF
    for k, (upper, lower) in enumerate(
        ((top, bottom), (pltpu.roll(top, C, 1), pltpu.roll(bottom, C, 1)))
    ):
        weight_ref[k, 0:HALF, :] = upper[:HALF, :C]
        weight_ref[k, HALF:C, :] = lower[:rest, :C]
        weight_ref[2, k * (C // 2) : (k + 1) * (C // 2), :] = lower[rest:HALF, :C]
    bias_ref[...] = top[HALF : HALF + 1, :C]


def call(kernel, out, specs, scratch, flops, moved, places=None, aliases=None):
    return pl.pallas_call(
        kernel,
        out_shape=[jax.ShapeDtypeStruct(s, d) for s, d in out],
        in_specs=specs,
        out_specs=places or [VMEM] * len(out),
        input_output_aliases=aliases or {},
        scratch_shapes=scratch,
        compiler_params=pltpu.CompilerParams(vmem_limit_bytes=24 * 1024 * 1024),
        cost_estimate=pl.CostEstimate(flops=flops, bytes_accessed=moved, transcendentals=0),
    )


def index(a, b, c, s):
    return ((a * SHAPE[1] + b) * SHAPE[2] + c) * SHAPE[3] + s


def place(i):
    return (i // 64, (i // 8) % 8, (i // 2) % 4, i % 2)


COUNT = 256
IN_CHIP = [(i, i ^ 1) for i in range(COUNT)]
CROSS = [(i, (i + 1) % COUNT) if i % 2 else (i, (i - 1) % COUNT) for i in range(COUNT)]
RING4 = ((1, 0, 3, 2), (3, 2, 1, 0))
PAIRS = (1, 0, 3, 2, 5, 4, 7, 6)
FAR = (5, 4, 7, 6, 1, 0, 3, 2)
NEXT = (6, 3, 0, 5, 2, 7, 4, 1)
NEAR = (7, 2, 1, 4, 3, 6, 5, 0)


def along(axis, table):
    pairs = []
    for i in range(COUNT):
        at = list(place(i))
        at[axis] = table[at[axis]]
        pairs.append((i, index(*at)))
    return pairs


def sent(value, pairs):
    return lax.ppermute(value, AXES, pairs)


def shards(features, lap_tiles, columns, weights, bias_term, cotangent):
    scale = 1.0 / math.sqrt(BATCH * PB * BLOCKS)
    field = ((ROWS, W2), F32)
    half = ((ROWS // 2, W2), F32)
    extended = ((EXT * PB, W2), F32)
    sums = ((2 * HALF + 8, W2), F32)
    share = ((HALF + 8, W2), F32)
    natural = ((MID, 2 * PB, NB * PB), BF16)
    turned = ((MID, NB * PB, 2 * PB), BF16)
    raw = ((NB, BLK_DEV // 8, CHUNKS * 8, 128), F32)
    cat = pltpu.VMEM((EXT * PB, 2 * W2), BF16)
    half_scratch = pltpu.VMEM((ROWS // 2, W2), F32)

    def scaled(kernel):
        def body(*refs):
            kernel(*refs, scale=scale)

        return body

    in_hbm = [
        pltpu.with_memory_space_constraint(value, pltpu.HBM)
        for value in (columns.T, jnp.transpose(lap_tiles, (1, 0, 2)), cotangent, features)
    ]
    cols, raw, fa_rim, at_rim, acc, s_a, s_b = call(
        rim_kernel,
        [((NB, BLK_DEV), jnp.int32), raw, natural, turned, extended, half, half],
        [HBM] * 4,
        [
            pltpu.SMEM((NB, BLK_DEV), jnp.int32), half_scratch, half_scratch,
            pltpu.SemaphoreType.DMA((2 * CHUNKS,)), pltpu.SemaphoreType.DMA((6,)),
        ],
        400_000_000, 4_000_000,
    )(*in_hbm)
    r_b = sent(s_b, CROSS)
    r_a = sent(s_a, IN_CHIP)
    catted = ((EXT * PB, 2 * W2), BF16)
    fa_mid, at_mid, f_mid, u_mid, u_rim, part, own_x = call(
        scaled(mid_kernel), [natural, turned, half, half, half, sums, catted],
        [SMEM] + [VMEM] * 4, [pltpu.VMEM(*extended)], 1_600_000_000, 9_000_000,
    )(cols, raw, cotangent, features, acc)
    f_rim, u_rim, keep, give, _ = call(
        scaled(meet_kernel), [half, half, share, share, catted], [SMEM] + [VMEM] * 7, [],
        400_000_000, 3_000_000, aliases={2: 4},
    )(cols, fa_rim, own_x, r_a, r_b, cotangent, u_rim, part)
    grads = keep + sent(give, IN_CHIP)
    (acc,) = call(
        inner_mid_kernel, [extended], [SMEM] + [VMEM] * 4, [half_scratch],
        400_000_000, 3_000_000,
    )(cols, at_mid, cotangent, u_mid, weights)
    u2, s_a, s_b = call(
        inner_rim_kernel, [field, half, half], [SMEM] + [VMEM] * 6,
        [half_scratch, pltpu.VMEM(*extended)], 400_000_000, 3_000_000,
    )(cols, at_rim, cotangent, u_rim, weights, f_rim, acc)
    s_b = sent(s_b, CROSS)
    s_a = sent(s_a, IN_CHIP)
    bias_row = bias_term.reshape(1, C)
    scratch = [cat, half_scratch, half_scratch, half_scratch]
    output, input_grad = call(
        last_mid_kernel, [field, field], [SMEM] + [VMEM] * 8,
        scratch + [pltpu.SemaphoreType.DMA((2,))], 600_000_000, 4_000_000, places=[HBM, HBM],
    )(cols, fa_mid, features, cotangent, f_mid, f_rim, u2, weights, bias_row)
    output, input_grad = call(
        last_rim_kernel, [field, field], [SMEM] + [VMEM] * 10 + [HBM, HBM],
        scratch + [pltpu.SemaphoreType.DMA((4,))], 600_000_000, 5_000_000,
        places=[HBM, HBM], aliases={11: 0, 12: 1},
    )(
        cols, fa_rim, features, cotangent, f_mid, f_rim, s_a, s_b, u2, weights, bias_row,
        output, input_grad,
    )
    grads = grads + sent(grads, along(2, RING4[0]))
    grads = grads + sent(grads, along(2, RING4[1]))
    grads = grads + sent(grads, along(0, RING4[0]))
    grads = grads + sent(grads, along(0, RING4[1]))
    grads = grads + sent(grads, along(1, PAIRS))
    far = sent(grads, along(1, FAR))
    following = sent(grads, along(1, NEXT))
    near = sent(grads, along(1, NEAR))
    (grads,) = call(pairs_kernel, [share], [VMEM] * 5, [], 1000, 100_000)(
        cols, grads, near, following, far
    )
    theirs = sent(grads, IN_CHIP)
    weight_grad, bias_grad = call(
        final_kernel, [((3, C, C), F32), ((1, C), F32)], [VMEM] * 3, [],
        1000, 100_000,
    )(cols, grads, theirs)
    return output, input_grad, weight_grad, bias_grad.reshape(C)


def solution(mesh):
    grid = Mesh(mesh.devices.reshape(*SHAPE), AXES)
    placed = (P(AXES, None), P(AXES, None, None), P(AXES, None), P(), P(), P(AXES, None))

    return jax.shard_map(
        shards,
        mesh=grid,
        in_specs=placed,
        out_specs=(P(AXES, None), P(AXES, None), P(), P()),
        check_vma=False,
    )
```

profile of v0, /device:TPU:1, one launch (start us, length us, event | category | flops | bytes accessed | tf_op | source)
XLA Modules:
  0.0 66.6 jit_solution(15253918127674782543)
XLA Ops:
  0.7 3.5 %shard_map.93 = (s32[6,16]{1,0:T(8,128)S(1)}, f32[6,2,256,128]{3,2,1,0:T(8,128)S(1)}, bf16[8,128,384]{2,1,0:T(8,128)(2,1)S(1)}, bf16[8,384,128]{2,1,0:T(8,128)(2...) custom-call(s32[6,16]{1,0:T(8,128)} %bitcast.7, f32[6,16,4096]{2,1,0:T(8,128)} %bitcast.6, ...), custom_call_target="tpu_custom_call" | custom-call | flops 400000000 | bytes 4000000 | tf_op jit(solution)/shard_map/pallas_call | solution.py:462
  4.1 3.3 %collective-permute-start = (f32[512,128]{1,0:T(8,128)S(1)}, f32[512,128]{1,0:T(8,128)S(1)}, u32[]{:S(2)}, u32[]{:S(2)}) collective-permute-start(f32[512,128]{1,0:T(8,128)S(1)} %get-tuple-element.37), channel_id=1, source_target_pairs={{0,1},{1,0},{2,3},{3,2},{4,5},{5,4},{6,7},{7,6},{8,9},{9,8},{10,11... | collective-permute-start | bytes 786440 | tf_op jit(solution)/shard_map/ppermute | solution.py:436
  7.4 0.0 collective-permute-start.1
  7.4 0.0 copy-start.2
  7.4 3.2 %shard_map.94 = (bf16[8,128,384]{2,1,0:T(8,128)(2,1)S(1)}, bf16[8,384,128]{2,1,0:T(8,128)(2,1)S(1)}, f32[512,128]{1,0:T(8,128)S(1)}, f32[512,128]{1,0:T(8,128)S(...) custom-call(s32[6,16]{1,0:T(8,128)S(1)} %get-tuple-element.31.refs_0_.cols, ...), custom_call_target="tpu_custom_call" | custom-call | flops 1600000000 | bytes 9000000 | tf_op jit(solution)/shard_map/pallas_call | solution.py:475
  10.6 1.6 %shard_map.96.acc_in = f32[1536,128]{1,0:T(8,128)S(1)} custom-call(s32[6,16]{1,0:T(8,128)S(1)} %get-tuple-element.31.refs_0_.cols, bf16[8,384,128]{2,1,0:T(8,128)(2,1)S(1)} %get-tuple-element.44.at_ref, f32[1024,128]{1,0:T(8,128)S(1)} %copy-done, f32[512,128]{1,0:T(8,128)S(1)} %get-tuple-element.45.u_ref, f32[3,64,64]{2,1,0:T(8,128)S(1)} %copy-done.2), custom_call_target="tpu_custom_call" | custom-call | flops 400000000 | bytes 3000000 | tf_op jit(solution)/shard_map/pallas_call | solution.py:484
  12.2 0.0 collective-permute-done.refs_3_
  12.2 1.0 %collective-permute-done.1.refs_4_ = f32[512,128]{1,0:T(8,128)S(1)} collective-permute-done((f32[512,128]{1,0:T(8,128)S(1)}, f32[512,128]{1,0:T(8,128)S(1)}, u32[]{:S(2)}, u32[]{:S(2)}) %collective-permute-start.1) | collective-permute-done | bytes 262176 | tf_op jit(solution)/shard_map/ppermute | solution.py:436
  13.2 1.6 %shard_map.95 = (f32[512,128]{1,0:T(8,128)S(1)}, f32[512,128]{1,0:T(8,128)S(1)}, f32[56,128]{1,0:T(8,128)S(1)}, f32[56,128]{1,0:T(8,128)S(1)}, bf16[1536,256]{1,0:T(8,128)(2,1)S(1)}) custom-call(s32[6,16]{1,0:T(8,128)S(1)} %get-tuple-element.31.refs_0_.cols, ...), custom_call_target="tpu_custom_call", output_to_operand_aliasing={{4}: (2, {})} | custom-call | flops 400000000 | bytes 3000000 | tf_op jit(solution)/shard_map/pallas_call | solution.py:479
  14.8 0.0 copy-start.3
  14.8 1.6 %shard_map.97 = (f32[1024,128]{1,0:T(8,128)S(1)}, f32[512,128]{1,0:T(8,128)S(1)}, f32[512,128]{1,0:T(8,128)S(1)}) custom-call(s32[6,16]{1,0:T(8,128)S(1)} %get-tuple-element.31.refs_0_.cols, bf16[8,384,128]{2,1,0:T(8,128)(2,1)S(1)} %get-tuple-element.42.at_ref, f32[1024,128]{1,0:T(8,128)S(1)} %copy-done, f32[512,128]{1,0:T(8,128)S(1)} %get-tuple-element.43.u_ref, ...), custom_call_target="tpu_custom_call" | custom-call | flops 400000000 | bytes 3000000 | tf_op jit(solution)/shard_map/pallas_call | solution.py:488
  16.4 8.0 %collective-permute-start.2 = (f32[512,128]{1,0:T(8,128)S(1)}, f32[512,128]{1,0:T(8,128)S(1)}, u32[]{:S(2)}, u32[]{:S(2)}) collective-permute-start(f32[512,128]{1,0:T(8,128)S(1)} %get-tuple-element.46), channel_id=1, source_target_pairs={{0,1},{1,0},{2,3},{3,2},{4,5},{5,4},{6,7},{7,6},{8,9},{9,8},{10,11... | collective-permute-start | bytes 786440 | tf_op jit(solution)/shard_map/ppermute | solution.py:436
  24.4 6.5 %collective-permute-start.4 = (f32[56,128]{1,0:T(8,128)S(1)}, f32[56,128]{1,0:T(8,128)S(1)}, u32[]{:S(2)}, u32[]{:S(2)}) collective-permute-start(f32[56,128]{1,0:T(8,128)S(1)} %get-tuple-element.55), channel_id=1, source_target_pairs={{0,1},{1,0},{2,3},{3,2},{4,5},{5,4},{6,7},{7,6},{8,9},{9,8},{10,11... | collective-permute-start | bytes 86024 | tf_op jit(solution)/shard_map/ppermute | solution.py:436
  30.9 0.9 %collective-permute-done.4 = f32[56,128]{1,0:T(8,128)S(1)} collective-permute-done((f32[56,128]{1,0:T(8,128)S(1)}, f32[56,128]{1,0:T(8,128)S(1)}, u32[]{:S(2)}, u32[]{:S(2)}) %collective-permute-start.4) | collective-permute-done | bytes 28704 | tf_op jit(solution)/shard_map/ppermute | solution.py:436
  31.8 3.0 %collective-permute-done.5 = f32[56,128]{1,0:T(8,128)S(1)} collective-permute-done((f32[56,128]{1,0:T(8,128)S(1)}, f32[56,128]{1,0:T(8,128)S(1)}, u32[]{:S(2)}, u32[]{:S(2)}) %collective-permute-start.5) | collective-permute-done | bytes 28704 | tf_op jit(solution)/shard_map/ppermute | solution.py:436
  34.8 0.0 collective-permute-start.6
  34.8 3.9 %collective-permute-done.6 = f32[56,128]{1,0:T(8,128)S(1)} collective-permute-done((f32[56,128]{1,0:T(8,128)S(1)}, f32[56,128]{1,0:T(8,128)S(1)}, u32[]{:S(2)}, u32[]{:S(2)}) %collective-permute-start.6) | collective-permute-done | bytes 28704 | tf_op jit(solution)/shard_map/ppermute | solution.py:436
  38.8 2.7 %collective-permute-done.7 = f32[56,128]{1,0:T(8,128)S(1)} collective-permute-done((f32[56,128]{1,0:T(8,128)S(1)}, f32[56,128]{1,0:T(8,128)S(1)}, u32[]{:S(2)}, u32[]{:S(2)}) %collective-permute-start.7) | collective-permute-done | bytes 28704 | tf_op jit(solution)/shard_map/ppermute | solution.py:436
  41.5 0.0 collective-permute-start.8
  41.5 3.9 %collective-permute-done.8 = f32[56,128]{1,0:T(8,128)S(1)} collective-permute-done((f32[56,128]{1,0:T(8,128)S(1)}, f32[56,128]{1,0:T(8,128)S(1)}, u32[]{:S(2)}, u32[]{:S(2)}) %collective-permute-start.8) | collective-permute-done | bytes 28704 | tf_op jit(solution)/shard_map/ppermute | solution.py:436
  45.4 2.7 %collective-permute-done.9 = f32[56,128]{1,0:T(8,128)S(1)} collective-permute-done((f32[56,128]{1,0:T(8,128)S(1)}, f32[56,128]{1,0:T(8,128)S(1)}, u32[]{:S(2)}, u32[]{:S(2)}) %collective-permute-start.9) | collective-permute-done | bytes 28704 | tf_op jit(solution)/shard_map/ppermute | solution.py:436
  48.2 0.0 collective-permute-start.12
  48.2 0.3 collective-permute-start.11
  48.4 2.4 %collective-permute-start.10 = (f32[56,128]{1,0:T(8,128)S(1)}, f32[56,128]{1,0:T(8,128)S(1)}, u32[]{:S(2)}, u32[]{:S(2)}) collective-permute-start(f32[56,128]{1,0:T(8,128)S(1)} %add.23.own), channel_id=1, source_target_pairs={{0,56},{1,57},{2,58},{3,59},{4,60},{5,61},{6,62},{7,63},{8,16},{9,... | collective-permute-start | bytes 86024 | tf_op jit(solution)/shard_map/ppermute | solution.py:436
  50.8 3.1 %collective-permute-done.12.far = f32[56,128]{1,0:T(8,128)S(1)} collective-permute-done((f32[56,128]{1,0:T(8,128)S(1)}, f32[56,128]{1,0:T(8,128)S(1)}, u32[]{:S(2)}, u32[]{:S(2)}) %collective-permute-start.12) | collective-permute-done | bytes 28704 | tf_op jit(solution)/shard_map/ppermute | solution.py:436
  53.9 0.0 collective-permute-done.11.following
  53.9 0.0 collective-permute-done.10.near
  53.9 0.1 shard_map.100.mine
  54.0 7.0 %collective-permute-start.13 = (f32[56,128]{1,0:T(8,128)S(1)}, f32[56,128]{1,0:T(8,128)S(1)}, u32[]{:S(2)}, u32[]{:S(2)}) collective-permute-start(f32[56,128]{1,0:T(8,128)S(1)} %shard_map.100.mine), channel_id=1, source_target_pairs={{0,1},{1,0},{2,3},{3,2},{4,5},{5,4},{6,7},{7,6},{8,9},{9,8},{10,11... | collective-permute-start | bytes 86024 | tf_op jit(solution)/shard_map/ppermute | solution.py:436
  61.0 2.3 %shard_map.98 = (f32[1024,128]{1,0:T(8,128)}, f32[1024,128]{1,0:T(8,128)}) custom-call(s32[6,16]{1,0:T(8,128)S(1)} %get-tuple-element.31.refs_0_.cols, bf16[8,128,384]{2,1,0:T(8,128)(2,1)S(1)} %get-tuple-element.49.fa_ref, f32[1024,128]{1,0:T(8,128)S(1)} %copy-done.1, f32[1024,128]{1,0:T(8,128)S(1)} %copy-done, f32[512,128]{1,0:T(8,128)S(1)} %get-tuple-element.35.f_mid, ...), custom_call_target="tpu_custom_call" | custom-call | flops 600000000 | bytes 4000000 | tf_op jit(solution)/shard_map/pallas_call | solution.py:496
  63.3 0.8 %shard_map.101 = (f32[3,64,64]{2,1,0:T(8,128)}, f32[1,64]{1,0:T(1,128)}) custom-call(s32[6,16]{1,0:T(8,128)S(1)} %get-tuple-element.31.refs_0_.cols, f32[56,128]{1,0:T(8,128)S(1)} %shard_map.100.mine, f32[56,128]{1,0:T(8,128)S(1)} %collective-permute-done.13.theirs), custom_call_target="tpu_custom_call" | custom-call | flops 1000 | bytes 100000 | tf_op jit(solution)/shard_map/pallas_call | solution.py:520
  64.1 2.4 %shard_map.99 = (f32[1024,128]{1,0:T(8,128)}, f32[1024,128]{1,0:T(8,128)}) custom-call(s32[6,16]{1,0:T(8,128)S(1)} %get-tuple-element.31.refs_0_.cols, bf16[8,128,384]{2,1,0:T(8,128)(2,1)S(1)} %get-tuple-element.32.refs_1_.fa_ref, f32[1024,128]{1,0:T(8,128)S(1)} %copy-done.1, ...), custom_call_target="tpu_custom_call", output_to_operand_aliasing={{0}: (11, {}), {1}: (12, {})} | custom-call | flops 600000000 | bytes 5000000 | tf_op jit(solution)/shard_map/pallas_call | solution.py:500
  (19 shorter events, 0.1 us)
Async XLA Ops:
  0.6 6.8 %copy-start = (f32[1024,128]{1,0:T(8,128)S(1)}, f32[1024,128]{1,0:T(8,128)}, u32[]{:S(2)}) copy-start(f32[1024,128]{1,0:T(8,128)} %g_ref.7) | copy-start | bytes 1572868
  0.6 6.8 %copy-start.1 = (f32[1024,128]{1,0:T(8,128)S(1)}, f32[1024,128]{1,0:T(8,128)}, u32[]{:S(2)}) copy-start(f32[1024,128]{1,0:T(8,128)} %x_ref.3) | copy-start | bytes 1572868
  4.1 8.1 %collective-permute-start = (f32[512,128]{1,0:T(8,128)S(1)}, f32[512,128]{1,0:T(8,128)S(1)}, u32[]{:S(2)}, u32[]{:S(2)}) collective-permute-start(f32[512,128]{1,0:T(8,128)S(1)} %get-tuple-element.37), channel_id=1, source_target_pairs={{0,1},{1,0},{2,3},{3,2},{4,5},{5,4},{6,7},{7,6},{8,9},{9,8},{10,11... | collective-permute-start | bytes 786440 | tf_op jit(solution)/shard_map/ppermute | solution.py:436
  7.4 5.8 %collective-permute-start.1 = (f32[512,128]{1,0:T(8,128)S(1)}, f32[512,128]{1,0:T(8,128)S(1)}, u32[]{:S(2)}, u32[]{:S(2)}) collective-permute-start(f32[512,128]{1,0:T(8,128)S(1)} %get-tuple-element.38), channel_id=1, source_target_pairs={{0,255},{1,2},{2,1},{3,4},{4,3},{5,6},{6,5},{7,8},{8,7},{9,10},{10... | collective-permute-start | bytes 786440 | tf_op jit(solution)/shard_map/ppermute | solution.py:436
  7.4 3.2 %copy-start.2 = (f32[3,64,64]{2,1,0:T(8,128)S(1)}, f32[3,64,64]{2,1,0:T(8,128)}, u32[]{:S(2)}) copy-start(f32[3,64,64]{2,1,0:T(8,128)} %w_ref.7) | copy-start | bytes 147460
  14.8 46.2 %copy-start.3 = (f32[64]{0:T(128)S(1)}, f32[64]{0:T(128)}, u32[]{:S(2)}) copy-start(f32[64]{0:T(128)} %param.10) | copy-start | bytes 772
  16.4 47.6 %collective-permute-start.2 = (f32[512,128]{1,0:T(8,128)S(1)}, f32[512,128]{1,0:T(8,128)S(1)}, u32[]{:S(2)}, u32[]{:S(2)}) collective-permute-start(f32[512,128]{1,0:T(8,128)S(1)} %get-tuple-element.46), channel_id=1, source_target_pairs={{0,1},{1,0},{2,3},{3,2},{4,5},{5,4},{6,7},{7,6},{8,9},{9,8},{10,11... | collective-permute-start | bytes 786440 | tf_op jit(solution)/shard_map/ppermute | solution.py:436
  24.4 39.7 %collective-permute-start.3 = (f32[512,128]{1,0:T(8,128)S(1)}, f32[512,128]{1,0:T(8,128)S(1)}, u32[]{:S(2)}, u32[]{:S(2)}) collective-permute-start(f32[512,128]{1,0:T(8,128)S(1)} %get-tuple-element.47), channel_id=1, source_target_pairs={{0,255},{1,2},{2,1},{3,4},{4,3},{5,6},{6,5},{7,8},{8,7},{9,10},{10... | collective-permute-start | bytes 786440 | tf_op jit(solution)/shard_map/ppermute | solution.py:436
  24.4 7.4 %collective-permute-start.4 = (f32[56,128]{1,0:T(8,128)S(1)}, f32[56,128]{1,0:T(8,128)S(1)}, u32[]{:S(2)}, u32[]{:S(2)}) collective-permute-start(f32[56,128]{1,0:T(8,128)S(1)} %get-tuple-element.55), channel_id=1, source_target_pairs={{0,1},{1,0},{2,3},{3,2},{4,5},{5,4},{6,7},{7,6},{8,9},{9,8},{10,11... | collective-permute-start | bytes 86024 | tf_op jit(solution)/shard_map/ppermute | solution.py:436
  31.8 3.0 %collective-permute-start.5 = (f32[56,128]{1,0:T(8,128)S(1)}, f32[56,128]{1,0:T(8,128)S(1)}, u32[]{:S(2)}, u32[]{:S(2)}) collective-permute-start(f32[56,128]{1,0:T(8,128)S(1)} %add.18), channel_id=1, source_target_pairs={{0,2},{1,3},{2,0},{3,1},{4,6},{5,7},{6,4},{7,5},{8,10},{9,11},{10,... | collective-permute-start | bytes 86024 | tf_op jit(solution)/shard_map/ppermute | solution.py:436
  34.8 3.9 %collective-permute-start.6 = (f32[56,128]{1,0:T(8,128)S(1)}, f32[56,128]{1,0:T(8,128)S(1)}, u32[]{:S(2)}, u32[]{:S(2)}) collective-permute-start(f32[56,128]{1,0:T(8,128)S(1)} %add.19), channel_id=1, source_target_pairs={{0,6},{1,7},{2,4},{3,5},{4,2},{5,3},{6,0},{7,1},{8,14},{9,15},{10,... | collective-permute-start | bytes 86024 | tf_op jit(solution)/shard_map/ppermute | solution.py:436
  38.8 2.7 %collective-permute-start.7 = (f32[56,128]{1,0:T(8,128)S(1)}, f32[56,128]{1,0:T(8,128)S(1)}, u32[]{:S(2)}, u32[]{:S(2)}) collective-permute-start(f32[56,128]{1,0:T(8,128)S(1)} %add.20), channel_id=1, source_target_pairs={{0,64},{1,65},{2,66},{3,67},{4,68},{5,69},{6,70},{7,71},{8,72},{9,... | collective-permute-start | bytes 86024 | tf_op jit(solution)/shard_map/ppermute | solution.py:436
  41.5 3.9 %collective-permute-start.8 = (f32[56,128]{1,0:T(8,128)S(1)}, f32[56,128]{1,0:T(8,128)S(1)}, u32[]{:S(2)}, u32[]{:S(2)}) collective-permute-start(f32[56,128]{1,0:T(8,128)S(1)} %add.21), channel_id=1, source_target_pairs={{0,192},{1,193},{2,194},{3,195},{4,196},{5,197},{6,198},{7,199},{8... | collective-permute-start | bytes 86024 | tf_op jit(solution)/shard_map/ppermute | solution.py:436
  45.4 2.7 %collective-permute-start.9 = (f32[56,128]{1,0:T(8,128)S(1)}, f32[56,128]{1,0:T(8,128)S(1)}, u32[]{:S(2)}, u32[]{:S(2)}) collective-permute-start(f32[56,128]{1,0:T(8,128)S(1)} %add.22), channel_id=1, source_target_pairs={{0,8},{1,9},{2,10},{3,11},{4,12},{5,13},{6,14},{7,15},{8,0},{9,1},... | collective-permute-start | bytes 86024 | tf_op jit(solution)/shard_map/ppermute | solution.py:436
  48.2 5.7 %collective-permute-start.12 = (f32[56,128]{1,0:T(8,128)S(1)}, f32[56,128]{1,0:T(8,128)S(1)}, u32[]{:S(2)}, u32[]{:S(2)}) collective-permute-start(f32[56,128]{1,0:T(8,128)S(1)} %add.23.own), channel_id=1, source_target_pairs={{0,40},{1,41},{2,42},{3,43},{4,44},{5,45},{6,46},{7,47},{8,32},{9,... | collective-permute-start | bytes 86024 | tf_op jit(solution)/shard_map/ppermute | solution.py:436
  48.2 5.7 %collective-permute-start.11 = (f32[56,128]{1,0:T(8,128)S(1)}, f32[56,128]{1,0:T(8,128)S(1)}, u32[]{:S(2)}, u32[]{:S(2)}) collective-permute-start(f32[56,128]{1,0:T(8,128)S(1)} %add.23.own), channel_id=1, source_target_pairs={{0,48},{1,49},{2,50},{3,51},{4,52},{5,53},{6,54},{7,55},{8,24},{9,... | collective-permute-start | bytes 86024 | tf_op jit(solution)/shard_map/ppermute | solution.py:436
  48.4 5.5 %collective-permute-start.10 = (f32[56,128]{1,0:T(8,128)S(1)}, f32[56,128]{1,0:T(8,128)S(1)}, u32[]{:S(2)}, u32[]{:S(2)}) collective-permute-start(f32[56,128]{1,0:T(8,128)S(1)} %add.23.own), channel_id=1, source_target_pairs={{0,56},{1,57},{2,58},{3,59},{4,60},{5,61},{6,62},{7,63},{8,16},{9,... | collective-permute-start | bytes 86024 | tf_op jit(solution)/shard_map/ppermute | solution.py:436
  54.0 9.3 %collective-permute-start.13 = (f32[56,128]{1,0:T(8,128)S(1)}, f32[56,128]{1,0:T(8,128)S(1)}, u32[]{:S(2)}, u32[]{:S(2)}) collective-permute-start(f32[56,128]{1,0:T(8,128)S(1)} %shard_map.100.mine), channel_id=1, source_target_pairs={{0,1},{1,0},{2,3},{3,2},{4,5},{5,4},{6,7},{7,6},{8,9},{9,8},{10,11... | collective-permute-start | bytes 86024 | tf_op jit(solution)/shard_map/ppermute | solution.py:436
where the time goes:
time: 66.7 us; the launch traced here: 66.6 us
  starting transfers between devices  27.5 us (41%)
  waiting for transfers between devices  21.2 us (32%)
  Pallas kernels  16.9 us (25%)
  between operations  0.97 us (1%)
    ppermute x14, starting transfers between devices, sent(): return lax.ppermute(value, AXES, pairs)  27.5 us
    ppermute x14, waiting for transfers between devices, sent(): return lax.ppermute(value, AXES, pairs)  21.2 us
    pallas_call x1, Pallas kernels, shards(): call(rim_kernel, [((NB, BLK_DEV), jnp.int32), raw, natural, turned, exten...  3.48 us
    pallas_call x1, Pallas kernels, shards(): call(scaled(mid_kernel), [natural, turned, half, half, half, sums, catted...  3.15 us
    pallas_call x1, Pallas kernels, shards(): call(last_rim_kernel, [field, field], [SMEM] + [VMEM] * 10 + [HBM, HBM],...  2.38 us
    pallas_call x1, Pallas kernels, shards(): call(last_mid_kernel, [field, field], [SMEM] + [VMEM] * 8, scratch + [plt...  2.26 us
    pallas_call x1, Pallas kernels, shards(): call(inner_rim_kernel, [field, half, half], [SMEM] + [VMEM] * 6, [half_sc...  1.62 us
    pallas_call x1, Pallas kernels, shards(): call(scaled(meet_kernel), [half, half, share, share, catted], [SMEM] + [V...  1.56 us
  transfers between devices with their start and end apart: 14, of which 8 were waited for; matrix products, arithmetic and copies ran while one was open for 0% of the time, Pallas kernels for 12%

commit v1 on v0

--- a/solution.py
+++ b/solution.py
@@ -49,35 +49,34 @@
     return jnp.bitwise_and(cols[j, b] - cols[0, 0] + HB, BLOCKS - 1)
 
 
-def is_first_core(cols):
-    return jnp.bitwise_and(cols[0, 0] // BLK_DEV, 1) == 0
-
-
-def rim_rows(cols):
-    first = is_first_core(cols)
-    low, high = 0, (BLK_DEV + HB) * PB
-    return (
-        pl.multiple_of(jnp.where(first, high, low), RIM),
-        pl.multiple_of(jnp.where(first, low, high), RIM),
-    )
-
-
-def rim_half(row):
-    return pl.multiple_of(jnp.where(row == 0, 0, RIM), RIM)
-
-
-def rim_block(i):
-    return jnp.where(i < HB, i, i + MID)
+def strip_of(cols):
+    return jnp.bitwise_and(cols[0, 0] // BLK_DEV, 1)
+
+
+class Side:
+    def __init__(self, end):
+        self.own = pl.multiple_of(end * (ROWS - RIM), RIM)
+        self.slots = pl.multiple_of(self.own + RIM, RIM)
+        self.beyond = pl.multiple_of(end * ((BLK_DEV + HB) * PB), RIM)
+        self.half = pl.multiple_of(end * RIM, RIM)
+        self.first = end * (BLK_DEV - HB)
+
+    def block(self, i):
+        return self.first + i
+
+
+def both_sides(cols):
+    strip = strip_of(cols)
+    return Side(strip), Side(1 - strip)
 
 
 def mid_block(i):
     return i + HB
 
 
-def block_rows(ref, i):
+def block_rows(ref, at):
     return jnp.concatenate(
-        [ref[pl.ds(i * PB, PB // 2, stride=2), :], ref[pl.ds(i * PB + 1, PB // 2, stride=2), :]],
-        axis=0,
+        [ref[pl.ds(at, PB // 2, stride=2), :], ref[pl.ds(at + 1, PB // 2, stride=2), :]], axis=0
     )
 
 
@@ -85,10 +84,10 @@
     return pl.ds(pl.multiple_of(slot * PB, PB), PB)
 
 
-def spread(cols, at_ref, vec_ref, acc, block):
+def spread(cols, at_ref, vec_ref, acc, block, count=MID, start=0):
     def one(i, carry):
         b = block(i)
-        high, low = split(block_rows(vec_ref, i))
+        high, low = split(block_rows(vec_ref, start + i * PB))
         rhs = jnp.concatenate([high, high, low, low], axis=0)
         at = at_ref[i]
         out = mm(jnp.concatenate([at, at], axis=1), rhs)
@@ -97,21 +96,21 @@
             acc[rows, :] = acc[rows, :] + out[j * PB : (j + 1) * PB]
         return carry
 
-    lax.fori_loop(0, MID, one, 0, unroll=8)
-
-
-def hop(cols, fa_ref, cat, out_ref, block):
+    lax.fori_loop(0, count, one, 0, unroll=count)
+
+
+def hop(cols, fa_ref, cat, out_ref, block, count=MID, start=0):
     def one(i, carry):
         b = block(i)
         rhs = jnp.concatenate([cat[rows_of(slot_of(cols, b, j)), :] for j in range(NB)], axis=0)
         out = mm(fa_ref[i], rhs)
         out = out[:, :W2] + out[:, W2:]
         out = out[:PB] + out[PB:]
-        out_ref[pl.ds(i * PB, PB // 2, stride=2), :] = out[: PB // 2]
-        out_ref[pl.ds(i * PB + 1, PB // 2, stride=2), :] = out[PB // 2 :]
+        out_ref[pl.ds(start + i * PB, PB // 2, stride=2), :] = out[: PB // 2]
+        out_ref[pl.ds(start + i * PB + 1, PB // 2, stride=2), :] = out[PB // 2 :]
         return carry
 
-    lax.fori_loop(0, MID, one, 0, unroll=8)
+    lax.fori_loop(0, count, one, 0, unroll=count)
 
 
 def put_cat(cat, start, value):
@@ -119,7 +118,7 @@
     cat[pl.ds(start, value.shape[0]), :] = jnp.concatenate([high, low], axis=1)
 
 
-def build(raw, fa_ref, at_ref, block, start=0, stop=MID):
+def build(raw, fa_ref, at_ref, block, count=MID):
     low_lanes = lax.broadcasted_iota(jnp.int32, (CHUNKS, 128), 1) < PB
 
     def one(i, carry):
@@ -139,50 +138,58 @@
             at_ref[i, lanes, :] = stacked.T
         return carry
 
-    lax.fori_loop(start, stop, one, 0, unroll=4)
-
-
-def rim_kernel(
+    lax.fori_loop(0, count, one, 0, unroll=4)
+
+
+def far_kernel(
     cols_hbm, tiles, g_hbm, x_hbm,
-    cols_ref, raw, fa_ref, at_ref, acc, send_a, send_b,
-    cols, g_rim, x_rim, sem, small,
+    cols_ref, raw, fa_ref, at_ref, acc, send,
+    cols, g_rim, sem, small,
 ):
-    to_cols = pltpu.make_async_copy(cols_hbm, cols, small.at[0])
-    others = [pltpu.make_async_copy(cols_hbm, cols_ref, small.at[1])]
-    for n, (value, to) in enumerate(((g_hbm, g_rim), (x_hbm, x_rim))):
-        others.append(
-            pltpu.make_async_copy(value.at[pl.ds(0, RIM)], to.at[pl.ds(0, RIM)], small.at[2 + 2 * n])
-        )
-        others.append(
+    strip = lax.axis_index("strip")
+    side = Side(strip)
+
+    def group_copies(group, n):
+        return [
             pltpu.make_async_copy(
-                value.at[pl.ds(ROWS - RIM, RIM)], to.at[pl.ds(RIM, RIM)], small.at[3 + 2 * n]
+                tiles.at[:, pl.ds(pl.multiple_of(8 * group, 8), 8), pl.ds(k * 128, 128)],
+                raw.at[:, group, pl.ds(8 * k, 8), :],
+                sem.at[n * CHUNKS + k],
             )
-        )
-    copies = [
-        pltpu.make_async_copy(
-            tiles.at[:, pl.ds(8 * group, 8), pl.ds(k * 128, 128)],
-            raw.at[:, group, pl.ds(8 * k, 8), :],
-            sem.at[group * CHUNKS + k],
-        )
-        for group in range(BLK_DEV // 8)
-        for k in range(CHUNKS)
+            for k in range(CHUNKS)
+        ]
+
+    now, later = group_copies(strip, 0), group_copies(1 - strip, 1)
+    rows = pl.ds(side.own, RIM)
+    soon = [
+        pltpu.make_async_copy(cols_hbm, cols, small.at[0]),
+        pltpu.make_async_copy(g_hbm.at[rows], g_rim, small.at[1]),
     ]
-    for copy in copies + [to_cols] + others:
+    late = [
+        pltpu.make_async_copy(cols_hbm, cols_ref, small.at[2]),
+        pltpu.make_async_copy(x_hbm.at[rows], send.at[pl.ds(0, RIM)], small.at[3]),
+    ]
+    for copy in now + soon + late + later:
         copy.start()
     acc[...] = jnp.zeros_like(acc)
-    for copy in copies[:CHUNKS]:
+    for copy in now:
         copy.wait()
-    build(raw, fa_ref, at_ref, rim_block, 0, HB)
-    for copy in copies[CHUNKS:]:
+    build(raw, fa_ref, at_ref, side.block, HB)
+    for copy in soon:
         copy.wait()
-    build(raw, fa_ref, at_ref, rim_block, HB, MID)
-    to_cols.wait()
-    for copy in others:
+    spread(cols, at_ref, g_rim, acc, side.block, HB)
+    send[RIM : 2 * RIM, :] = acc[pl.ds(side.beyond, RIM), :]
+    for copy in late + later:
         copy.wait()
-    spread(cols, at_ref, g_rim, acc, rim_block)
-    for row, send in zip(rim_rows(cols), (send_a, send_b)):
-        send[0:RIM, :] = x_rim[pl.ds(rim_half(row), RIM), :]
-        send[RIM : 2 * RIM, :] = acc[pl.ds(row, RIM), :]
+
+
+def near_kernel(cols, raw, g_ref, x_ref, acc_in, fa_ref, at_ref, acc, send):
+    del acc_in
+    _, side = both_sides(cols)
+    build(raw, fa_ref, at_ref, side.block, HB)
+    spread(cols, at_ref, g_ref, acc, side.block, HB, side.own)
+    send[0:RIM, :] = x_ref[pl.ds(side.own, RIM), :]
+    send[RIM : 2 * RIM, :] = acc[pl.ds(side.beyond, RIM), :]
 
 
 def maps_sum(full):
@@ -234,7 +241,7 @@
 
 def mid_kernel(
     cols, raw, g_ref, x_ref, acc_in,
-    fa_ref, at_ref, first_ref, u_mid, u_rim, part_ref, cat,
+    fa_ref, at_ref, first_ref, u_mid, u_b, u_a, part_ref, cat,
     acc, *, scale,
 ):
     put_cat(cat, RIM, x_ref[...])
@@ -243,8 +250,8 @@
     g_mid = g_ref.at[pl.ds(RIM, MID * PB)]
     spread(cols, at_ref, g_mid, acc, mid_block)
     u_mid[...] = acc[2 * RIM : 4 * RIM, :]
-    u_rim[0:RIM, :] = acc[RIM : 2 * RIM, :]
-    u_rim[RIM : 2 * RIM, :] = acc[4 * RIM : 5 * RIM, :]
+    for side, u in zip(both_sides(cols), (u_b, u_a)):
+        u[...] = acc[pl.ds(side.slots, RIM), :]
     hop(cols, fa_ref, cat, first_ref, mid_block)
     ((zero,),) = products([x_ref[...]], [g_ref[...]])
     ((one, two),) = products([first_ref[...]], [g_mid[...], u_mid[...]])
@@ -253,22 +260,28 @@
     part_ref[C + C // 2 :, :] = jnp.broadcast_to(bias + pltpu.roll(bias, C, 1), (8, 128))
 
 
+def side_rows(ref, sides):
+    return jnp.concatenate([ref[pl.ds(side.own, RIM), :] for side in sides], axis=0)
+
+
 def meet_kernel(
-    cols, fa_ref, cat_in, r_a, r_b, g_ref, u_part, part_ref,
-    first_ref, u_ref, keep_ref, give_ref, cat, *, scale
+    cols, fa_b, fa_a, cat_in, r_b, r_a, g_ref, p_b, p_a, part_ref,
+    f_b, f_a, u_b, u_a, keep_ref, give_ref, cat, *, scale
 ):
     del cat_in
-    for row, r in zip(rim_rows(cols), (r_a, r_b)):
-        put_cat(cat, row, r[0:RIM, :])
-        half = pl.ds(rim_half(row), RIM)
-        u_ref[half, :] = u_part[half, :] + r[RIM : 2 * RIM, :]
-    hop(cols, fa_ref, cat, first_ref, rim_block)
-    g_rim = jnp.concatenate([g_ref[0:RIM, :], g_ref[ROWS - RIM :, :]], axis=0)
-    ((one, two),) = products([first_ref[...]], [g_rim, u_ref[...]])
+    sides = both_sides(cols)
+    for side, r, p, u in zip(sides, (r_b, r_a), (p_b, p_a), (u_b, u_a)):
+        put_cat(cat, side.beyond, r[0:RIM, :])
+        u[...] = p[...] + r[RIM : 2 * RIM, :]
+    for side, fa_ref, first in zip(sides, (fa_b, fa_a), (f_b, f_a)):
+        hop(cols, fa_ref, cat, first, side.block, HB)
+    first = jnp.concatenate([f_b[...], f_a[...]], axis=0)
+    u = jnp.concatenate([u_b[...], u_a[...]], axis=0)
+    ((one, two),) = products([first], [side_rows(g_ref, sides), u])
     total = part_ref[0 : 2 * HALF, :] + scale * packed(None, one, 2.0 * two)
-    first = is_first_core(cols)
-    keep_ref[0:HALF, :] = jnp.where(first, total[:HALF], total[HALF:])
-    give_ref[0:HALF, :] = jnp.where(first, total[HALF:], total[:HALF])
+    lower = strip_of(cols) == 0
+    keep_ref[0:HALF, :] = jnp.where(lower, total[:HALF], total[HALF:])
+    give_ref[0:HALF, :] = jnp.where(lower, total[HALF:], total[:HALF])
     keep_ref[HALF:, :] = part_ref[2 * HALF :, :]
     give_ref[HALF:, :] = part_ref[2 * HALF :, :]
 
@@ -284,16 +297,19 @@
 
 
 def inner_rim_kernel(
-    cols, at_ref, g_ref, u_ref, w_ref, first_ref, acc_in, u2_ref, send_a, send_b, inner, acc
+    cols, at_b, at_a, g_ref, u_b, u_a, w_ref, f_b, f_a, acc_in,
+    u2_ref, send_b, send_a, acc, inner,
 ):
-    g_rim = jnp.concatenate([g_ref[0:RIM, :], g_ref[ROWS - RIM :, :]], axis=0)
-    inner[...] = inner_rows(g_rim, u_ref[...], w_ref)
-    acc[...] = acc_in[...]
-    spread(cols, at_ref, inner, acc, rim_block)
+    del acc_in
+    sides = both_sides(cols)
+    u = jnp.concatenate([u_b[...], u_a[...]], axis=0)
+    inner[...] = inner_rows(side_rows(g_ref, sides), u, w_ref)
+    for n, (side, at_ref) in enumerate(zip(sides, (at_b, at_a))):
+        spread(cols, at_ref, inner, acc, side.block, HB, n * RIM)
     u2_ref[...] = acc[RIM : RIM + ROWS, :]
-    for row, send in zip(rim_rows(cols), (send_a, send_b)):
-        send[0:RIM, :] = first_ref[pl.ds(rim_half(row), RIM), :]
-        send[RIM : 2 * RIM, :] = acc[pl.ds(row, RIM), :]
+    for side, first, send in zip(sides, (f_b, f_a), (send_b, send_a)):
+        send[0:RIM, :] = first[...]
+        send[RIM : 2 * RIM, :] = acc[pl.ds(side.beyond, RIM), :]
 
 
 def outputs(x, g, one, hopped, w_ref, bias_ref):
@@ -307,17 +323,17 @@
     return out, mixed(g, both_maps(w_ref[0] - w_ref[2]).T)
 
 
-def own_cat(cat, f_mid, f_rim):
-    put_cat(cat, RIM, f_rim[0:RIM, :])
+def own_cat(cols, cat, f_mid, f_b, f_a):
     put_cat(cat, 2 * RIM, f_mid[...])
-    put_cat(cat, 4 * RIM, f_rim[RIM : 2 * RIM, :])
+    for side, first in zip(both_sides(cols), (f_b, f_a)):
+        put_cat(cat, side.slots, first[...])
 
 
 def last_mid_kernel(
-    cols, fa_ref, x_ref, g_ref, f_mid, f_rim, u2_ref, w_ref, bias_ref,
+    cols, fa_ref, x_ref, g_ref, f_mid, f_b, f_a, u2_ref, w_ref, bias_ref,
     out_hbm, back_hbm, cat, second, out_ref, back_ref, sem,
 ):
-    own_cat(cat, f_mid, f_rim)
+    own_cat(cols, cat, f_mid, f_b, f_a)
     hop(cols, fa_ref, cat, second, mid_block)
     mid = slice(RIM, ROWS - RIM)
     out, back = outputs(x_ref[mid, :], g_ref[mid, :], f_mid[...], second[...], w_ref, bias_ref)
@@ -334,22 +350,25 @@
 
 
 def last_rim_kernel(
-    cols, fa_ref, x_ref, g_ref, f_mid, f_rim, r_a, r_b, u2_ref, w_ref, bias_ref, o_in, b_in,
+    cols, fa_b, fa_a, x_ref, g_ref, f_mid, f_b, f_a, r_b, r_a, u2_ref, w_ref, bias_ref, o_in, b_in,
     out_hbm, back_hbm, cat, second, out_ref, back_ref, sem,
 ):
     del o_in, b_in
-    own_cat(cat, f_mid, f_rim)
-    for row, r in zip(rim_rows(cols), (r_a, r_b)):
-        put_cat(cat, row, r[0:RIM, :])
-    hop(cols, fa_ref, cat, second, rim_block)
-    x = jnp.concatenate([x_ref[0:RIM, :], x_ref[ROWS - RIM :, :]], axis=0)
-    g = jnp.concatenate([g_ref[0:RIM, :], g_ref[ROWS - RIM :, :]], axis=0)
-    out, back = outputs(x, g, f_rim[...], second[...], w_ref, bias_ref)
-    out_ref[...] = out
-    back_ref[...] = back + jnp.concatenate([u2_ref[0:RIM, :], u2_ref[ROWS - RIM :, :]], axis=0)
-    for row, r in zip(rim_rows(cols), (r_a, r_b)):
-        half = pl.ds(rim_half(row), RIM)
-        back_ref[half, :] = back_ref[half, :] + r[RIM : 2 * RIM, :]
+    sides = both_sides(cols)
+    own_cat(cols, cat, f_mid, f_b, f_a)
+    for side, r in zip(sides, (r_b, r_a)):
+        put_cat(cat, side.beyond, r[0:RIM, :])
+    for n, (side, fa_ref) in enumerate(zip(sides, (fa_b, fa_a))):
+        hop(cols, fa_ref, cat, second, side.block, HB, n * RIM)
+    first = jnp.concatenate([f_b[...], f_a[...]], axis=0)
+    out, back = outputs(
+        side_rows(x_ref, sides), side_rows(g_ref, sides), first, second[...], w_ref, bias_ref
+    )
+    back = back + side_rows(u2_ref, sides)
+    for n, (side, r) in enumerate(zip(sides, (r_b, r_a))):
+        half = pl.ds(side.half, RIM)
+        out_ref[half, :] = out[n * RIM : (n + 1) * RIM]
+        back_ref[half, :] = back[n * RIM : (n + 1) * RIM] + r[RIM : 2 * RIM, :]
     copies = [
         pltpu.make_async_copy(
             value.at[pl.ds(n * RIM, RIM)], to.at[pl.ds(n * (ROWS - RIM), RIM)], sem.at[2 * k + n]
@@ -459,50 +478,57 @@
         pltpu.with_memory_space_constraint(value, pltpu.HBM)
         for value in (columns.T, jnp.transpose(lap_tiles, (1, 0, 2)), cotangent, features)
     ]
-    cols, raw, fa_rim, at_rim, acc, s_a, s_b = call(
-        rim_kernel,
-        [((NB, BLK_DEV), jnp.int32), raw, natural, turned, extended, half, half],
+    quarter = ((RIM, W2), F32)
+    natural_4 = ((HB, 2 * PB, NB * PB), BF16)
+    turned_4 = ((HB, NB * PB, 2 * PB), BF16)
+    cols, raw, fa_b, at_b, acc, s_b = call(
+        far_kernel,
+        [((NB, BLK_DEV), jnp.int32), raw, natural_4, turned_4, extended, half],
         [HBM] * 4,
         [
-            pltpu.SMEM((NB, BLK_DEV), jnp.int32), half_scratch, half_scratch,
-            pltpu.SemaphoreType.DMA((2 * CHUNKS,)), pltpu.SemaphoreType.DMA((6,)),
+            pltpu.SMEM((NB, BLK_DEV), jnp.int32), pltpu.VMEM(*quarter),
+            pltpu.SemaphoreType.DMA((2 * CHUNKS,)), pltpu.SemaphoreType.DMA((4,)),
         ],
-        400_000_000, 4_000_000,
+        200_000_000, 3_000_000,
     )(*in_hbm)
     r_b = sent(s_b, CROSS)
+    fa_a, at_a, acc, s_a = call(
+        near_kernel, [natural_4, turned_4, extended, half], [SMEM] + [VMEM] * 4, [],
+        200_000_000, 3_000_000, aliases={4: 2},
+    )(cols, raw, cotangent, features, acc)
     r_a = sent(s_a, IN_CHIP)
     catted = ((EXT * PB, 2 * W2), BF16)
-    fa_mid, at_mid, f_mid, u_mid, u_rim, part, own_x = call(
-        scaled(mid_kernel), [natural, turned, half, half, half, sums, catted],
+    fa_mid, at_mid, f_mid, u_mid, u_b, u_a, part, own_x = call(
+        scaled(mid_kernel), [natural, turned, half, half, quarter, quarter, sums, catted],
         [SMEM] + [VMEM] * 4, [pltpu.VMEM(*extended)], 1_600_000_000, 9_000_000,
     )(cols, raw, cotangent, features, acc)
-    f_rim, u_rim, keep, give, _ = call(
-        scaled(meet_kernel), [half, half, share, share, catted], [SMEM] + [VMEM] * 7, [],
-        400_000_000, 3_000_000, aliases={2: 4},
-    )(cols, fa_rim, own_x, r_a, r_b, cotangent, u_rim, part)
+    f_b, f_a, u_b, u_a, keep, give, _ = call(
+        scaled(meet_kernel), [quarter] * 4 + [share, share, catted],
+        [SMEM] + [VMEM] * 9, [], 400_000_000, 3_000_000, aliases={3: 6},
+    )(cols, fa_b, fa_a, own_x, r_b, r_a, cotangent, u_b, u_a, part)
     grads = keep + sent(give, IN_CHIP)
     (acc,) = call(
         inner_mid_kernel, [extended], [SMEM] + [VMEM] * 4, [half_scratch],
         400_000_000, 3_000_000,
     )(cols, at_mid, cotangent, u_mid, weights)
-    u2, s_a, s_b = call(
-        inner_rim_kernel, [field, half, half], [SMEM] + [VMEM] * 6,
-        [half_scratch, pltpu.VMEM(*extended)], 400_000_000, 3_000_000,
-    )(cols, at_rim, cotangent, u_rim, weights, f_rim, acc)
+    u2, s_b, s_a, _ = call(
+        inner_rim_kernel, [field, half, half, extended], [SMEM] + [VMEM] * 9,
+        [half_scratch], 400_000_000, 3_000_000, aliases={9: 3},
+    )(cols, at_b, at_a, cotangent, u_b, u_a, weights, f_b, f_a, acc)
     s_b = sent(s_b, CROSS)
     s_a = sent(s_a, IN_CHIP)
     bias_row = bias_term.reshape(1, C)
     scratch = [cat, half_scratch, half_scratch, half_scratch]
     output, input_grad = call(
-        last_mid_kernel, [field, field], [SMEM] + [VMEM] * 8,
+        last_mid_kernel, [field, field], [SMEM] + [VMEM] * 9,
         scratch + [pltpu.SemaphoreType.DMA((2,))], 600_000_000, 4_000_000, places=[HBM, HBM],
-    )(cols, fa_mid, features, cotangent, f_mid, f_rim, u2, weights, bias_row)
+    )(cols, fa_mid, features, cotangent, f_mid, f_b, f_a, u2, weights, bias_row)
     output, input_grad = call(
-        last_rim_kernel, [field, field], [SMEM] + [VMEM] * 10 + [HBM, HBM],
+        last_rim_kernel, [field, field], [SMEM] + [VMEM] * 12 + [HBM, HBM],
         scratch + [pltpu.SemaphoreType.DMA((4,))], 600_000_000, 5_000_000,
-        places=[HBM, HBM], aliases={11: 0, 12: 1},
+        places=[HBM, HBM], aliases={13: 0, 14: 1},
     )(
-        cols, fa_rim, features, cotangent, f_mid, f_rim, s_a, s_b, u2, weights, bias_row,
+        cols, fa_b, fa_a, features, cotangent, f_mid, f_b, f_a, s_b, s_a, u2, weights, bias_row,
         output, input_grad,
     )
     grads = grads + sent(grads, along(2, RING4[0]))

time: 66.7 us -> 65.5 us (0.982)
  starting transfers between devices: 27.5 us -> 26.5 us
    ppermute x14, starting transfers between devices: 27.5 us -> 26.5 us  [sent(): return lax.ppermute(value, AXES, pairs)]
    ppermute x14, waiting for transfers between devices: 21.2 us -> 20.6 us  [sent(): return lax.ppermute(value, AXES, pairs)]
    pallas_call x6 -> x7, Pallas kernels: 14.5 us -> 14.9 us  [the longest x1 3.15 us: shards(): call(scaled(mid_kernel), [natural, turned, half, half, quarter, quarter,...]
  transfers between devices with their start and end apart: 14 -> 14, of which waited for: 8 -> 7; matrix products, arithmetic and copies ran while one was open for 0% -> 0% of each run, Pallas kernels for 12% -> 14%
where the time goes in v1:
time: 65.5 us; the launch traced here: 65.4 us
  starting transfers between devices  26.5 us (40%)
  waiting for transfers between devices  20.6 us (31%)
  Pallas kernels  17.3 us (26%)
  between operations  0.98 us (1%)
    ppermute x14, starting transfers between devices, sent(): return lax.ppermute(value, AXES, pairs)  26.5 us
    ppermute x14, waiting for transfers between devices, sent(): return lax.ppermute(value, AXES, pairs)  20.6 us
    pallas_call x1, Pallas kernels, shards(): call(scaled(mid_kernel), [natural, turned, half, half, quarter, quarter,...  3.15 us
    pallas_call x1, Pallas kernels, shards(): call(far_kernel, [((NB, BLK_DEV), jnp.int32), raw, natural_4, turned_4, e...  2.74 us
    pallas_call x1, Pallas kernels, shards(): call(last_rim_kernel, [field, field], [SMEM] + [VMEM] * 12 + [HBM, HBM],...  2.33 us
    pallas_call x1, Pallas kernels, shards(): call(last_mid_kernel, [field, field], [SMEM] + [VMEM] * 9, scratch + [plt...  2.26 us
    pallas_call x1, Pallas kernels, shards(): call(inner_rim_kernel, [field, half, half, extended], [SMEM] + [VMEM] * 9...  1.62 us
    pallas_call x1, Pallas kernels, shards(): call(inner_mid_kernel, [extended], [SMEM] + [VMEM] * 4, [half_scratch], 4...  1.55 us
  transfers between devices with their start and end apart: 14, of which 7 were waited for; matrix products, arithmetic and copies ran while one was open for 0% of the time, Pallas kernels for 14%

profile of v1, /device:TPU:1, one launch (start us, length us, event | category | flops | bytes accessed | tf_op | source)
XLA Modules:
  0.0 65.4 jit_solution(17215335592447559798)
XLA Ops:
  0.7 2.7 %shard_map.93 = (s32[6,16]{1,0:T(8,128)S(1)}, f32[6,2,256,128]{3,2,1,0:T(8,128)S(1)}, bf16[4,128,384]{2,1,0:T(8,128)(2,1)S(1)}, bf16[4,384,128]{2,1,0:T(8,128)(2...) custom-call(s32[6,16]{1,0:T(8,128)} %bitcast.7, f32[6,16,4096]{2,1,0:T(8,128)} %bitcast.6, f32[1024,128]{1,0:T(8,128)} %g_ref.9, ...), custom_call_target="tpu_custom_call" | custom-call | flops 200000000 | bytes 3000000 | tf_op jit(solution)/shard_map/pallas_call | solution.py:484
  3.4 2.8 %collective-permute-start = (f32[512,128]{1,0:T(8,128)S(1)}, f32[512,128]{1,0:T(8,128)S(1)}, u32[]{:S(2)}, u32[]{:S(2)}) collective-permute-start(f32[512,128]{1,0:T(8,128)S(1)} %get-tuple-element.45), channel_id=1, source_target_pairs={{0,255},{1,2},{2,1},{3,4},{4,3},{5,6},{6,5},{7,8},{8,7},{9,10},{10... | collective-permute-start | bytes 786440 | tf_op jit(solution)/shard_map/ppermute | solution.py:455
  6.2 1.3 %shard_map.94 = (bf16[4,128,384]{2,1,0:T(8,128)(2,1)S(1)}, bf16[4,384,128]{2,1,0:T(8,128)(2,1)S(1)}, f32[1536,128]{1,0:T(8,128)S(1)}, f32[512,128]{1,0:T(8,128)S(1)}) custom-call(s32[6,16]{1,0:T(8,128)S(1)} %get-tuple-element.37.cols.refs_0_, f32[6,2,256,128]{3,2,1,0:T(8,128)S(1)} %get-tuple-element.39.raw.refs_1_, ...), custom_call_target="tpu_custom_call", output_to_operand_aliasing={{2}: (4, {})} | custom-call | flops 200000000 | bytes 3000000 | tf_op jit(solution)/shard_map/pallas_call | solution.py:495
  7.4 8.9 %collective-permute-start.1 = (f32[512,128]{1,0:T(8,128)S(1)}, f32[512,128]{1,0:T(8,128)S(1)}, u32[]{:S(2)}, u32[]{:S(2)}) collective-permute-start(f32[512,128]{1,0:T(8,128)S(1)} %get-tuple-element.46), channel_id=1, source_target_pairs={{0,1},{1,0},{2,3},{3,2},{4,5},{5,4},{6,7},{7,6},{8,9},{9,8},{10,11... | collective-permute-start | bytes 786440 | tf_op jit(solution)/shard_map/ppermute | solution.py:455
  16.3 3.1 %shard_map.95 = (bf16[8,128,384]{2,1,0:T(8,128)(2,1)S(1)}, bf16[8,384,128]{2,1,0:T(8,128)(2,1)S(1)}, f32[512,128]{1,0:T(8,128)S(1)}, f32[512,128]{1,0:T(8,128)S(...) custom-call(s32[6,16]{1,0:T(8,128)S(1)} %get-tuple-element.37.cols.r, ...), custom_call_target="tpu_custom_call" | custom-call | flops 1600000000 | bytes 9000000 | tf_op jit(solution)/shard_map/pallas_call | solution.py:501
  19.5 1.5 %shard_map.97.acc_in = f32[1536,128]{1,0:T(8,128)S(1)} custom-call(s32[6,16]{1,0:T(8,128)S(1)} %get-tuple-element.37.cols.refs_0_, bf16[8,384,128]{2,1,0:T(8,128)(2,1)S(1)} %get-tuple-element.56.at_ref, f32[1024,128]{1,0:T(8,128)S(1)} %copy-done, f32[512,128]{1,0:T(8,128)S(1)} %get-tuple-element.57.u_ref, f32[3,64,64]{2,1,0:T(8,128)S(1)} %copy-done.2), custom_call_target="tpu_custom_call" | custom-call | flops 400000000 | bytes 3000000 | tf_op jit(solution)/shard_map/pallas_call | solution.py:510
  21.0 0.0 collective-permute-done.refs_4_
  21.0 1.5 %shard_map.96 = (f32[256,128]{1,0:T(8,128)S(1)}, f32[256,128]{1,0:T(8,128)S(1)}, f32[256,128]{1,0:T(8,128)S(1)}, f32[256,128]{1,0:T(8,128)S(1)}, f32[56,128]{1,0...) custom-call(s32[6,16]{1,0:T(8,128)S(1)} %get-tuple-element.37.cols.refs_0_, ...), custom_call_target="tpu_custom_call", output_to_operand_aliasing={{6}: (3, {})} | custom-call | flops 400000000 | bytes 3000000 | tf_op jit(solution)/shard_map/pallas_call | solution.py:505
  22.6 0.0 copy-start.3
  22.6 1.6 %shard_map.98 = (f32[1024,128]{1,0:T(8,128)S(1)}, f32[512,128]{1,0:T(8,128)S(1)}, f32[512,128]{1,0:T(8,128)S(1)}, f32[1536,128]{1,0:T(8,128)S(1)}) custom-call(s32[6,16]{1,0:T(8,128)S(1)} %get-tuple-element.37.cols.refs_0_, bf16[4,384,128]{2,1,0:T(8,128)(2,1)S(1)} %get-tuple-element.52.at_b, ...), custom_call_target="tpu_custom_call", output_to_operand_aliasing={{3}: (9, {})} | custom-call | flops 400000000 | bytes 3000000 | tf_op jit(solution)/shard_map/pallas_call | solution.py:514
  24.2 0.1 collective-permute-start.2
  24.3 5.1 %collective-permute-start.3 = (f32[512,128]{1,0:T(8,128)S(1)}, f32[512,128]{1,0:T(8,128)S(1)}, u32[]{:S(2)}, u32[]{:S(2)}) collective-permute-start(f32[512,128]{1,0:T(8,128)S(1)} %get-tuple-element.59), channel_id=1, source_target_pairs={{0,1},{1,0},{2,3},{3,2},{4,5},{5,4},{6,7},{7,6},{8,9},{9,8},{10,11... | collective-permute-start | bytes 786440 | tf_op jit(solution)/shard_map/ppermute | solution.py:455
  29.4 0.0 collective-permute-start.4
  29.4 1.2 %collective-permute-done.4 = f32[56,128]{1,0:T(8,128)S(1)} collective-permute-done((f32[56,128]{1,0:T(8,128)S(1)}, f32[56,128]{1,0:T(8,128)S(1)}, u32[]{:S(2)}, u32[]{:S(2)}) %collective-permute-start.4) | collective-permute-done | bytes 28704 | tf_op jit(solution)/shard_map/ppermute | solution.py:455
  30.6 0.0 collective-permute-start.5
  30.6 3.0 %collective-permute-done.5 = f32[56,128]{1,0:T(8,128)S(1)} collective-permute-done((f32[56,128]{1,0:T(8,128)S(1)}, f32[56,128]{1,0:T(8,128)S(1)}, u32[]{:S(2)}, u32[]{:S(2)}) %collective-permute-start.5) | collective-permute-done | bytes 28704 | tf_op jit(solution)/shard_map/ppermute | solution.py:455
  33.6 0.0 collective-permute-start.6
  33.7 3.9 %collective-permute-done.6 = f32[56,128]{1,0:T(8,128)S(1)} collective-permute-done((f32[56,128]{1,0:T(8,128)S(1)}, f32[56,128]{1,0:T(8,128)S(1)}, u32[]{:S(2)}, u32[]{:S(2)}) %collective-permute-start.6) | collective-permute-done | bytes 28704 | tf_op jit(solution)/shard_map/ppermute | solution.py:455
  37.6 0.0 collective-permute-start.7
  37.6 2.7 %collective-permute-done.7 = f32[56,128]{1,0:T(8,128)S(1)} collective-permute-done((f32[56,128]{1,0:T(8,128)S(1)}, f32[56,128]{1,0:T(8,128)S(1)}, u32[]{:S(2)}, u32[]{:S(2)}) %collective-permute-start.7) | collective-permute-done | bytes 28704 | tf_op jit(solution)/shard_map/ppermute | solution.py:455
  40.3 0.0 collective-permute-start.8
  40.3 3.9 %collective-permute-done.8 = f32[56,128]{1,0:T(8,128)S(1)} collective-permute-done((f32[56,128]{1,0:T(8,128)S(1)}, f32[56,128]{1,0:T(8,128)S(1)}, u32[]{:S(2)}, u32[]{:S(2)}) %collective-permute-start.8) | collective-permute-done | bytes 28704 | tf_op jit(solution)/shard_map/ppermute | solution.py:455
  44.3 0.0 collective-permute-start.9
  44.3 2.7 %collective-permute-done.9 = f32[56,128]{1,0:T(8,128)S(1)} collective-permute-done((f32[56,128]{1,0:T(8,128)S(1)}, f32[56,128]{1,0:T(8,128)S(1)}, u32[]{:S(2)}, u32[]{:S(2)}) %collective-permute-start.9) | collective-permute-done | bytes 28704 | tf_op jit(solution)/shard_map/ppermute | solution.py:455
  47.0 0.3 collective-permute-start.11
  47.3 2.4 %collective-permute-start.10 = (f32[56,128]{1,0:T(8,128)S(1)}, f32[56,128]{1,0:T(8,128)S(1)}, u32[]{:S(2)}, u32[]{:S(2)}) collective-permute-start(f32[56,128]{1,0:T(8,128)S(1)} %add.23.own), channel_id=1, source_target_pairs={{0,56},{1,57},{2,58},{3,59},{4,60},{5,61},{6,62},{7,63},{8,16},{9,... | collective-permute-start | bytes 86024 | tf_op jit(solution)/shard_map/ppermute | solution.py:455
  49.6 3.1 %collective-permute-done.12.far = f32[56,128]{1,0:T(8,128)S(1)} collective-permute-done((f32[56,128]{1,0:T(8,128)S(1)}, f32[56,128]{1,0:T(8,128)S(1)}, u32[]{:S(2)}, u32[]{:S(2)}) %collective-permute-start.12) | collective-permute-done | bytes 28704 | tf_op jit(solution)/shard_map/ppermute | solution.py:455
  52.7 0.1 shard_map.101.mine
  52.8 7.1 %collective-permute-start.13 = (f32[56,128]{1,0:T(8,128)S(1)}, f32[56,128]{1,0:T(8,128)S(1)}, u32[]{:S(2)}, u32[]{:S(2)}) collective-permute-start(f32[56,128]{1,0:T(8,128)S(1)} %shard_map.101.mine), channel_id=1, source_target_pairs={{0,1},{1,0},{2,3},{3,2},{4,5},{5,4},{6,7},{7,6},{8,9},{9,8},{10,11... | collective-permute-start | bytes 86024 | tf_op jit(solution)/shard_map/ppermute | solution.py:455
  59.9 2.3 %shard_map.99 = (f32[1024,128]{1,0:T(8,128)}, f32[1024,128]{1,0:T(8,128)}) custom-call(s32[6,16]{1,0:T(8,128)S(1)} %get-tuple-element.37.cols.refs_0_, bf16[8,128,384]{2,1,0:T(8,128)(2,1)S(1)} %get-tuple-element.61.fa_ref, f32[1024,128]{1,0:T(8,128)S(1)} %copy-done.1, f32[1024,128]{1,0:T(8,128)S(1)} %copy-done, f32[512,128]{1,0:T(8,128)S(1)} %get-tuple-element.43.f_mid, ...), custom_call_target="tpu_custom_call" | custom-call | flops 600000000 | bytes 4000000 | tf_op jit(solution)/shard_map/pallas_call | solution.py:522
  62.1 0.8 %shard_map.102 = (f32[3,64,64]{2,1,0:T(8,128)}, f32[1,64]{1,0:T(1,128)}) custom-call(s32[6,16]{1,0:T(8,128)S(1)} %get-tuple-element.37.cols.refs_0_, f32[56,128]{1,0:T(8,128)S(1)} %shard_map.101.mine, f32[56,128]{1,0:T(8,128)S(1)} %collective-permute-done.13.theirs), custom_call_target="tpu_custom_call" | custom-call | flops 1000 | bytes 100000 | tf_op jit(solution)/shard_map/pallas_call | solution.py:546
  62.9 2.3 %shard_map.100 = (f32[1024,128]{1,0:T(8,128)}, f32[1024,128]{1,0:T(8,128)}) custom-call(s32[6,16]{1,0:T(8,128)S(1)} %get-tuple-element.37.cols.refs_0_, bf16[4,128,384]{2,1,0:T(8,128)(2,1)S(1)} %get-tuple-element.38.refs_1_.fa_b, bf16[4,128,384]{2,1,0:T(8,128)(2,1)S(1)} %get-tuple-element.41.refs_2_.fa_a, ...), custom_call_target="tpu_custom_call", output_to_operand_aliasing={{0}: (13, {}), {1}: (14, {})} | custom-call | flops 600000000 | bytes 5000000 | tf_op jit(solution)/shard_map/pallas_call | solution.py:526
  (20 shorter events, 0.1 us)
Async XLA Ops:
  0.6 5.5 %copy-start = (f32[1024,128]{1,0:T(8,128)S(1)}, f32[1024,128]{1,0:T(8,128)}, u32[]{:S(2)}) copy-start(f32[1024,128]{1,0:T(8,128)} %g_ref.9) | copy-start | bytes 1572868
  0.6 5.5 %copy-start.1 = (f32[1024,128]{1,0:T(8,128)S(1)}, f32[1024,128]{1,0:T(8,128)}, u32[]{:S(2)}) copy-start(f32[1024,128]{1,0:T(8,128)} %x_ref.5) | copy-start | bytes 1572868
  3.4 17.6 %collective-permute-start = (f32[512,128]{1,0:T(8,128)S(1)}, f32[512,128]{1,0:T(8,128)S(1)}, u32[]{:S(2)}, u32[]{:S(2)}) collective-permute-start(f32[512,128]{1,0:T(8,128)S(1)} %get-tuple-element.45), channel_id=1, source_target_pairs={{0,255},{1,2},{2,1},{3,4},{4,3},{5,6},{6,5},{7,8},{8,7},{9,10},{10... | collective-permute-start | bytes 786440 | tf_op jit(solution)/shard_map/ppermute | solution.py:455
  7.4 13.6 %collective-permute-start.1 = (f32[512,128]{1,0:T(8,128)S(1)}, f32[512,128]{1,0:T(8,128)S(1)}, u32[]{:S(2)}, u32[]{:S(2)}) collective-permute-start(f32[512,128]{1,0:T(8,128)S(1)} %get-tuple-element.46), channel_id=1, source_target_pairs={{0,1},{1,0},{2,3},{3,2},{4,5},{5,4},{6,7},{7,6},{8,9},{9,8},{10,11... | collective-permute-start | bytes 786440 | tf_op jit(solution)/shard_map/ppermute | solution.py:455
  16.3 3.2 %copy-start.2 = (f32[3,64,64]{2,1,0:T(8,128)S(1)}, f32[3,64,64]{2,1,0:T(8,128)}, u32[]{:S(2)}) copy-start(f32[3,64,64]{2,1,0:T(8,128)} %w_ref.7) | copy-start | bytes 147460
  22.6 37.3 %copy-start.3 = (f32[64]{0:T(128)S(1)}, f32[64]{0:T(128)}, u32[]{:S(2)}) copy-start(f32[64]{0:T(128)} %param.10) | copy-start | bytes 772
  24.2 38.7 %collective-permute-start.2 = (f32[512,128]{1,0:T(8,128)S(1)}, f32[512,128]{1,0:T(8,128)S(1)}, u32[]{:S(2)}, u32[]{:S(2)}) collective-permute-start(f32[512,128]{1,0:T(8,128)S(1)} %get-tuple-element.58), channel_id=1, source_target_pairs={{0,255},{1,2},{2,1},{3,4},{4,3},{5,6},{6,5},{7,8},{8,7},{9,10},{10... | collective-permute-start | bytes 786440 | tf_op jit(solution)/shard_map/ppermute | solution.py:455
  24.3 38.6 %collective-permute-start.3 = (f32[512,128]{1,0:T(8,128)S(1)}, f32[512,128]{1,0:T(8,128)S(1)}, u32[]{:S(2)}, u32[]{:S(2)}) collective-permute-start(f32[512,128]{1,0:T(8,128)S(1)} %get-tuple-element.59), channel_id=1, source_target_pairs={{0,1},{1,0},{2,3},{3,2},{4,5},{5,4},{6,7},{7,6},{8,9},{9,8},{10,11... | collective-permute-start | bytes 786440 | tf_op jit(solution)/shard_map/ppermute | solution.py:455
  29.4 1.2 %collective-permute-start.4 = (f32[56,128]{1,0:T(8,128)S(1)}, f32[56,128]{1,0:T(8,128)S(1)}, u32[]{:S(2)}, u32[]{:S(2)}) collective-permute-start(f32[56,128]{1,0:T(8,128)S(1)} %get-tuple-element.67), channel_id=1, source_target_pairs={{0,1},{1,0},{2,3},{3,2},{4,5},{5,4},{6,7},{7,6},{8,9},{9,8},{10,11... | collective-permute-start | bytes 86024 | tf_op jit(solution)/shard_map/ppermute | solution.py:455
  30.6 3.0 %collective-permute-start.5 = (f32[56,128]{1,0:T(8,128)S(1)}, f32[56,128]{1,0:T(8,128)S(1)}, u32[]{:S(2)}, u32[]{:S(2)}) collective-permute-start(f32[56,128]{1,0:T(8,128)S(1)} %add.18), channel_id=1, source_target_pairs={{0,2},{1,3},{2,0},{3,1},{4,6},{5,7},{6,4},{7,5},{8,10},{9,11},{10,... | collective-permute-start | bytes 86024 | tf_op jit(solution)/shard_map/ppermute | solution.py:455
  33.6 3.9 %collective-permute-start.6 = (f32[56,128]{1,0:T(8,128)S(1)}, f32[56,128]{1,0:T(8,128)S(1)}, u32[]{:S(2)}, u32[]{:S(2)}) collective-permute-start(f32[56,128]{1,0:T(8,128)S(1)} %add.19), channel_id=1, source_target_pairs={{0,6},{1,7},{2,4},{3,5},{4,2},{5,3},{6,0},{7,1},{8,14},{9,15},{10,... | collective-permute-start | bytes 86024 | tf_op jit(solution)/shard_map/ppermute | solution.py:455
  37.6 2.7 %collective-permute-start.7 = (f32[56,128]{1,0:T(8,128)S(1)}, f32[56,128]{1,0:T(8,128)S(1)}, u32[]{:S(2)}, u32[]{:S(2)}) collective-permute-start(f32[56,128]{1,0:T(8,128)S(1)} %add.20), channel_id=1, source_target_pairs={{0,64},{1,65},{2,66},{3,67},{4,68},{5,69},{6,70},{7,71},{8,72},{9,... | collective-permute-start | bytes 86024 | tf_op jit(solution)/shard_map/ppermute | solution.py:455
  40.3 3.9 %collective-permute-start.8 = (f32[56,128]{1,0:T(8,128)S(1)}, f32[56,128]{1,0:T(8,128)S(1)}, u32[]{:S(2)}, u32[]{:S(2)}) collective-permute-start(f32[56,128]{1,0:T(8,128)S(1)} %add.21), channel_id=1, source_target_pairs={{0,192},{1,193},{2,194},{3,195},{4,196},{5,197},{6,198},{7,199},{8... | collective-permute-start | bytes 86024 | tf_op jit(solution)/shard_map/ppermute | solution.py:455
  44.3 2.7 %collective-permute-start.9 = (f32[56,128]{1,0:T(8,128)S(1)}, f32[56,128]{1,0:T(8,128)S(1)}, u32[]{:S(2)}, u32[]{:S(2)}) collective-permute-start(f32[56,128]{1,0:T(8,128)S(1)} %add.22), channel_id=1, source_target_pairs={{0,8},{1,9},{2,10},{3,11},{4,12},{5,13},{6,14},{7,15},{8,0},{9,1},... | collective-permute-start | bytes 86024 | tf_op jit(solution)/shard_map/ppermute | solution.py:455
  47.0 5.7 %collective-permute-start.12 = (f32[56,128]{1,0:T(8,128)S(1)}, f32[56,128]{1,0:T(8,128)S(1)}, u32[]{:S(2)}, u32[]{:S(2)}) collective-permute-start(f32[56,128]{1,0:T(8,128)S(1)} %add.23.own), channel_id=1, source_target_pairs={{0,40},{1,41},{2,42},{3,43},{4,44},{5,45},{6,46},{7,47},{8,32},{9,... | collective-permute-start | bytes 86024 | tf_op jit(solution)/shard_map/ppermute | solution.py:455
  47.0 5.7 %collective-permute-start.11 = (f32[56,128]{1,0:T(8,128)S(1)}, f32[56,128]{1,0:T(8,128)S(1)}, u32[]{:S(2)}, u32[]{:S(2)}) collective-permute-start(f32[56,128]{1,0:T(8,128)S(1)} %add.23.own), channel_id=1, source_target_pairs={{0,48},{1,49},{2,50},{3,51},{4,52},{5,53},{6,54},{7,55},{8,24},{9,... | collective-permute-start | bytes 86024 | tf_op jit(solution)/shard_map/ppermute | solution.py:455
  47.3 5.5 %collective-permute-start.10 = (f32[56,128]{1,0:T(8,128)S(1)}, f32[56,128]{1,0:T(8,128)S(1)}, u32[]{:S(2)}, u32[]{:S(2)}) collective-permute-start(f32[56,128]{1,0:T(8,128)S(1)} %add.23.own), channel_id=1, source_target_pairs={{0,56},{1,57},{2,58},{3,59},{4,60},{5,61},{6,62},{7,63},{8,16},{9,... | collective-permute-start | bytes 86024 | tf_op jit(solution)/shard_map/ppermute | solution.py:455
  52.8 9.3 %collective-permute-start.13 = (f32[56,128]{1,0:T(8,128)S(1)}, f32[56,128]{1,0:T(8,128)S(1)}, u32[]{:S(2)}, u32[]{:S(2)}) collective-permute-start(f32[56,128]{1,0:T(8,128)S(1)} %shard_map.101.mine), channel_id=1, source_target_pairs={{0,1},{1,0},{2,3},{3,2},{4,5},{5,4},{6,7},{7,6},{8,9},{9,8},{10,11... | collective-permute-start | bytes 86024 | tf_op jit(solution)/shard_map/ppermute | solution.py:455

commit v2 on v1

--- a/solution.py
+++ b/solution.py
@@ -138,7 +138,7 @@
             at_ref[i, lanes, :] = stacked.T
         return carry
 
-    lax.fori_loop(0, count, one, 0, unroll=4)
+    lax.fori_loop(0, count, one, 0, unroll=count)
 
 
 def far_kernel(
@@ -531,10 +531,14 @@
         cols, fa_b, fa_a, features, cotangent, f_mid, f_b, f_a, s_b, s_a, u2, weights, bias_row,
         output, input_grad,
     )
-    grads = grads + sent(grads, along(2, RING4[0]))
-    grads = grads + sent(grads, along(2, RING4[1]))
-    grads = grads + sent(grads, along(0, RING4[0]))
-    grads = grads + sent(grads, along(0, RING4[1]))
+    opposite = sent(grads, along(2, (2, 3, 0, 1)))
+    beside = sent(grads, along(2, RING4[0]))
+    other = sent(grads, along(2, RING4[1]))
+    grads = (grads + beside) + (other + opposite)
+    opposite = sent(grads, along(0, (2, 3, 0, 1)))
+    beside = sent(grads, along(0, RING4[0]))
+    other = sent(grads, along(0, RING4[1]))
+    grads = (grads + beside) + (other + opposite)
     grads = grads + sent(grads, along(1, PAIRS))
     far = sent(grads, along(1, FAR))
     following = sent(grads, along(1, NEXT))

time: 65.5 us -> 55 us (0.84)
  waiting for transfers between devices: 20.6 us -> 7.45 us
  starting transfers between devices: 26.5 us -> 29.5 us
    ppermute x14 -> x16, waiting for transfers between devices: 20.6 us -> 7.45 us  [sent(): return lax.ppermute(value, AXES, pairs)]
    ppermute x14 -> x16, starting transfers between devices: 26.5 us -> 29.5 us  [sent(): return lax.ppermute(value, AXES, pairs)]
  transfers between devices with their start and end apart: 14 -> 16, of which waited for: 7 -> 4; matrix products, arithmetic and copies ran while one was open for 0% -> 0% of each run, Pallas kernels for 14% -> 19%
where the time goes in v2:
time: 55 us; the launch traced here: 54.9 us
  starting transfers between devices  29.5 us (54%)
  Pallas kernels  17 us (31%)
  waiting for transfers between devices  7.45 us (14%)
  between operations  0.96 us (2%)
    ppermute x16, starting transfers between devices, sent(): return lax.ppermute(value, AXES, pairs)  29.5 us
    ppermute x16, waiting for transfers between devices, sent(): return lax.ppermute(value, AXES, pairs)  7.45 us
    pallas_call x1, Pallas kernels, shards(): call(scaled(mid_kernel), [natural, turned, half, half, quarter, quarter,...  2.81 us
    pallas_call x1, Pallas kernels, shards(): call(far_kernel, [((NB, BLK_DEV), jnp.int32), raw, natural_4, turned_4, e...  2.75 us
    pallas_call x1, Pallas kernels, shards(): call(last_rim_kernel, [field, field], [SMEM] + [VMEM] * 12 + [HBM, HBM],...  2.33 us
    pallas_call x1, Pallas kernels, shards(): call(last_mid_kernel, [field, field], [SMEM] + [VMEM] * 9, scratch + [plt...  2.26 us
    pallas_call x1, Pallas kernels, shards(): call(inner_rim_kernel, [field, half, half, extended], [SMEM] + [VMEM] * 9...  1.61 us
    pallas_call x1, Pallas kernels, shards(): call(inner_mid_kernel, [extended], [SMEM] + [VMEM] * 4, [half_scratch], 4...  1.56 us
  transfers between devices with their start and end apart: 16, of which 4 were waited for; matrix products, arithmetic and copies ran while one was open for 0% of the time, Pallas kernels for 19%

profile of v2, /device:TPU:1, one launch (start us, length us, event | category | flops | bytes accessed | tf_op | source)
XLA Modules:
  0.0 54.9 jit_solution(14688666443646144115)
XLA Ops:
  0.7 2.7 %shard_map.93 = (s32[6,16]{1,0:T(8,128)S(1)}, f32[6,2,256,128]{3,2,1,0:T(8,128)S(1)}, bf16[4,128,384]{2,1,0:T(8,128)(2,1)S(1)}, bf16[4,384,128]{2,1,0:T(8,128)(2...) custom-call(s32[6,16]{1,0:T(8,128)} %bitcast.7, f32[6,16,4096]{2,1,0:T(8,128)} %bitcast.6, f32[1024,128]{1,0:T(8,128)} %g_ref.9, ...), custom_call_target="tpu_custom_call" | custom-call | flops 200000000 | bytes 3000000 | tf_op jit(solution)/shard_map/pallas_call | solution.py:484
  3.4 2.8 %collective-permute-start = (f32[512,128]{1,0:T(8,128)S(1)}, f32[512,128]{1,0:T(8,128)S(1)}, u32[]{:S(2)}, u32[]{:S(2)}) collective-permute-start(f32[512,128]{1,0:T(8,128)S(1)} %get-tuple-element.45), channel_id=1, source_target_pairs={{0,255},{1,2},{2,1},{3,4},{4,3},{5,6},{6,5},{7,8},{8,7},{9,10},{10... | collective-permute-start | bytes 786440 | tf_op jit(solution)/shard_map/ppermute | solution.py:455
  6.2 1.3 %shard_map.94 = (bf16[4,128,384]{2,1,0:T(8,128)(2,1)S(1)}, bf16[4,384,128]{2,1,0:T(8,128)(2,1)S(1)}, f32[1536,128]{1,0:T(8,128)S(1)}, f32[512,128]{1,0:T(8,128)S(1)}) custom-call(s32[6,16]{1,0:T(8,128)S(1)} %get-tuple-element.37.cols.refs_0_, f32[6,2,256,128]{3,2,1,0:T(8,128)S(1)} %get-tuple-element.39.raw.refs_1_, ...), custom_call_target="tpu_custom_call", output_to_operand_aliasing={{2}: (4, {})} | custom-call | flops 200000000 | bytes 3000000 | tf_op jit(solution)/shard_map/pallas_call | solution.py:495
  7.4 8.8 %collective-permute-start.1 = (f32[512,128]{1,0:T(8,128)S(1)}, f32[512,128]{1,0:T(8,128)S(1)}, u32[]{:S(2)}, u32[]{:S(2)}) collective-permute-start(f32[512,128]{1,0:T(8,128)S(1)} %get-tuple-element.46), channel_id=1, source_target_pairs={{0,1},{1,0},{2,3},{3,2},{4,5},{5,4},{6,7},{7,6},{8,9},{9,8},{10,11... | collective-permute-start | bytes 786440 | tf_op jit(solution)/shard_map/ppermute | solution.py:455
  16.3 2.8 %shard_map.95 = (bf16[8,128,384]{2,1,0:T(8,128)(2,1)S(1)}, bf16[8,384,128]{2,1,0:T(8,128)(2,1)S(1)}, f32[512,128]{1,0:T(8,128)S(1)}, f32[512,128]{1,0:T(8,128)S(...) custom-call(s32[6,16]{1,0:T(8,128)S(1)} %get-tuple-element.37.cols.r, ...), custom_call_target="tpu_custom_call" | custom-call | flops 1600000000 | bytes 9000000 | tf_op jit(solution)/shard_map/pallas_call | solution.py:501
  19.1 0.0 collective-permute-done.refs_4_
  19.1 0.0 collective-permute-done.1.refs_5_
  19.1 1.5 %shard_map.96 = (f32[256,128]{1,0:T(8,128)S(1)}, f32[256,128]{1,0:T(8,128)S(1)}, f32[256,128]{1,0:T(8,128)S(1)}, f32[256,128]{1,0:T(8,128)S(1)}, f32[56,128]{1,0...) custom-call(s32[6,16]{1,0:T(8,128)S(1)} %get-tuple-element.37.cols.refs_0_, ...), custom_call_target="tpu_custom_call", output_to_operand_aliasing={{6}: (3, {})} | custom-call | flops 400000000 | bytes 3000000 | tf_op jit(solution)/shard_map/pallas_call | solution.py:505
  20.7 0.1 collective-permute-start.4
  20.8 1.2 %collective-permute-done.4 = f32[56,128]{1,0:T(8,128)S(1)} collective-permute-done((f32[56,128]{1,0:T(8,128)S(1)}, f32[56,128]{1,0:T(8,128)S(1)}, u32[]{:S(2)}, u32[]{:S(2)}) %collective-permute-start.4) | collective-permute-done | bytes 28704 | tf_op jit(solution)/shard_map/ppermute | solution.py:455
  22.0 0.1 collective-permute-start.6
  22.1 2.5 %collective-permute-start.5 = (f32[56,128]{1,0:T(8,128)S(1)}, f32[56,128]{1,0:T(8,128)S(1)}, u32[]{:S(2)}, u32[]{:S(2)}) collective-permute-start(f32[56,128]{1,0:T(8,128)S(1)} %add.24), channel_id=1, source_target_pairs={{0,2},{1,3},{2,0},{3,1},{4,6},{5,7},{6,4},{7,5},{8,10},{9,11},{10,... | collective-permute-start | bytes 86024 | tf_op jit(solution)/shard_map/ppermute | solution.py:455
  24.6 1.6 %shard_map.97.acc_in = f32[1536,128]{1,0:T(8,128)S(1)} custom-call(s32[6,16]{1,0:T(8,128)S(1)} %get-tuple-element.37.cols.refs_0_, bf16[8,384,128]{2,1,0:T(8,128)(2,1)S(1)} %get-tuple-element.56.at_ref, f32[1024,128]{1,0:T(8,128)S(1)} %copy-done, f32[512,128]{1,0:T(8,128)S(1)} %get-tuple-element.57.u_ref, f32[3,64,64]{2,1,0:T(8,128)S(1)} %copy-done.2), custom_call_target="tpu_custom_call" | custom-call | flops 400000000 | bytes 3000000 | tf_op jit(solution)/shard_map/pallas_call | solution.py:510
  26.2 0.1 collective-permute-done.7
  26.3 0.0 collective-permute-done.6
  26.3 0.0 copy-start.3
  26.3 0.6 %collective-permute-start.10 = (f32[56,128]{1,0:T(8,128)S(1)}, f32[56,128]{1,0:T(8,128)S(1)}, u32[]{:S(2)}, u32[]{:S(2)}) collective-permute-start(f32[56,128]{1,0:T(8,128)S(1)} %add_add_fusion.1), channel_id=1, source_target_pairs={{0,128},{1,129},{2,130},{3,131},{4,132},{5,133},{6,134},{7,135},{8... | collective-permute-start | bytes 86024 | tf_op jit(solution)/shard_map/ppermute | solution.py:455
  26.9 0.9 %collective-permute-start.9 = (f32[56,128]{1,0:T(8,128)S(1)}, f32[56,128]{1,0:T(8,128)S(1)}, u32[]{:S(2)}, u32[]{:S(2)}) collective-permute-start(f32[56,128]{1,0:T(8,128)S(1)} %add_add_fusion.1), channel_id=1, source_target_pairs={{0,192},{1,193},{2,194},{3,195},{4,196},{5,197},{6,198},{7,199},{8... | collective-permute-start | bytes 86024 | tf_op jit(solution)/shard_map/ppermute | solution.py:455
  27.8 1.3 %collective-permute-start.8 = (f32[56,128]{1,0:T(8,128)S(1)}, f32[56,128]{1,0:T(8,128)S(1)}, u32[]{:S(2)}, u32[]{:S(2)}) collective-permute-start(f32[56,128]{1,0:T(8,128)S(1)} %add_add_fusion.1), channel_id=1, source_target_pairs={{0,64},{1,65},{2,66},{3,67},{4,68},{5,69},{6,70},{7,71},{8,72},{9,... | collective-permute-start | bytes 86024 | tf_op jit(solution)/shard_map/ppermute | solution.py:455
  29.1 1.6 %shard_map.98 = (f32[1024,128]{1,0:T(8,128)S(1)}, f32[512,128]{1,0:T(8,128)S(1)}, f32[512,128]{1,0:T(8,128)S(1)}, f32[1536,128]{1,0:T(8,128)S(1)}) custom-call(s32[6,16]{1,0:T(8,128)S(1)} %get-tuple-element.37.cols.refs_0_, bf16[4,384,128]{2,1,0:T(8,128)(2,1)S(1)} %get-tuple-element.52.at_b, ...), custom_call_target="tpu_custom_call", output_to_operand_aliasing={{3}: (9, {})} | custom-call | flops 400000000 | bytes 3000000 | tf_op jit(solution)/shard_map/pallas_call | solution.py:514
  30.7 3.7 %collective-permute-start.2 = (f32[512,128]{1,0:T(8,128)S(1)}, f32[512,128]{1,0:T(8,128)S(1)}, u32[]{:S(2)}, u32[]{:S(2)}) collective-permute-start(f32[512,128]{1,0:T(8,128)S(1)} %get-tuple-element.58), channel_id=1, source_target_pairs={{0,255},{1,2},{2,1},{3,4},{4,3},{5,6},{6,5},{7,8},{8,7},{9,10},{10... | collective-permute-start | bytes 786440 | tf_op jit(solution)/shard_map/ppermute | solution.py:455
  34.4 3.4 %collective-permute-start.3 = (f32[512,128]{1,0:T(8,128)S(1)}, f32[512,128]{1,0:T(8,128)S(1)}, u32[]{:S(2)}, u32[]{:S(2)}) collective-permute-start(f32[512,128]{1,0:T(8,128)S(1)} %get-tuple-element.59), channel_id=1, source_target_pairs={{0,1},{1,0},{2,3},{3,2},{4,5},{5,4},{6,7},{7,6},{8,9},{9,8},{10,11... | collective-permute-start | bytes 786440 | tf_op jit(solution)/shard_map/ppermute | solution.py:455
  37.8 0.3 collective-permute-start.11
  38.1 3.0 %collective-permute-done.11 = f32[56,128]{1,0:T(8,128)S(1)} collective-permute-done((f32[56,128]{1,0:T(8,128)S(1)}, f32[56,128]{1,0:T(8,128)S(1)}, u32[]{:S(2)}, u32[]{:S(2)}) %collective-permute-start.11) | collective-permute-done | bytes 28704 | tf_op jit(solution)/shard_map/ppermute | solution.py:455
  41.1 0.1 collective-permute-start.13
  41.2 2.5 %collective-permute-start.12 = (f32[56,128]{1,0:T(8,128)S(1)}, f32[56,128]{1,0:T(8,128)S(1)}, u32[]{:S(2)}, u32[]{:S(2)}) collective-permute-start(f32[56,128]{1,0:T(8,128)S(1)} %add.31.own), channel_id=1, source_target_pairs={{0,56},{1,57},{2,58},{3,59},{4,60},{5,61},{6,62},{7,63},{8,16},{9,... | collective-permute-start | bytes 86024 | tf_op jit(solution)/shard_map/ppermute | solution.py:455
  43.7 3.1 %collective-permute-done.14.far = f32[56,128]{1,0:T(8,128)S(1)} collective-permute-done((f32[56,128]{1,0:T(8,128)S(1)}, f32[56,128]{1,0:T(8,128)S(1)}, u32[]{:S(2)}, u32[]{:S(2)}) %collective-permute-start.14) | collective-permute-done | bytes 28704 | tf_op jit(solution)/shard_map/ppermute | solution.py:455
  46.9 0.1 shard_map.101.mine
  46.9 2.4 %collective-permute-start.15 = (f32[56,128]{1,0:T(8,128)S(1)}, f32[56,128]{1,0:T(8,128)S(1)}, u32[]{:S(2)}, u32[]{:S(2)}) collective-permute-start(f32[56,128]{1,0:T(8,128)S(1)} %shard_map.101.mine), channel_id=1, source_target_pairs={{0,1},{1,0},{2,3},{3,2},{4,5},{5,4},{6,7},{7,6},{8,9},{9,8},{10,11... | collective-permute-start | bytes 86024 | tf_op jit(solution)/shard_map/ppermute | solution.py:455
  49.3 2.3 %shard_map.99 = (f32[1024,128]{1,0:T(8,128)}, f32[1024,128]{1,0:T(8,128)}) custom-call(s32[6,16]{1,0:T(8,128)S(1)} %get-tuple-element.37.cols.refs_0_, bf16[8,128,384]{2,1,0:T(8,128)(2,1)S(1)} %get-tuple-element.61.fa_ref, f32[1024,128]{1,0:T(8,128)S(1)} %copy-done.1, f32[1024,128]{1,0:T(8,128)S(1)} %copy-done, f32[512,128]{1,0:T(8,128)S(1)} %get-tuple-element.43.f_mid, ...), custom_call_target="tpu_custom_call" | custom-call | flops 600000000 | bytes 4000000 | tf_op jit(solution)/shard_map/pallas_call | solution.py:522
  51.6 0.8 %shard_map.102 = (f32[3,64,64]{2,1,0:T(8,128)}, f32[1,64]{1,0:T(1,128)}) custom-call(s32[6,16]{1,0:T(8,128)S(1)} %get-tuple-element.37.cols.refs_0_, f32[56,128]{1,0:T(8,128)S(1)} %shard_map.101.mine, f32[56,128]{1,0:T(8,128)S(1)} %collective-permute-done.15.theirs), custom_call_target="tpu_custom_call" | custom-call | flops 1000 | bytes 100000 | tf_op jit(solution)/shard_map/pallas_call | solution.py:550
  52.4 2.3 %shard_map.100 = (f32[1024,128]{1,0:T(8,128)}, f32[1024,128]{1,0:T(8,128)}) custom-call(s32[6,16]{1,0:T(8,128)S(1)} %get-tuple-element.37.cols.refs_0_, bf16[4,128,384]{2,1,0:T(8,128)(2,1)S(1)} %get-tuple-element.38.refs_1_.fa_b, bf16[4,128,384]{2,1,0:T(8,128)(2,1)S(1)} %get-tuple-element.41.refs_2_.fa_a, ...), custom_call_target="tpu_custom_call", output_to_operand_aliasing={{0}: (13, {}), {1}: (14, {})} | custom-call | flops 600000000 | bytes 5000000 | tf_op jit(solution)/shard_map/pallas_call | solution.py:526
  (22 shorter events, 0.1 us)
Async XLA Ops:
  0.6 5.5 %copy-start = (f32[1024,128]{1,0:T(8,128)S(1)}, f32[1024,128]{1,0:T(8,128)}, u32[]{:S(2)}) copy-start(f32[1024,128]{1,0:T(8,128)} %g_ref.9) | copy-start | bytes 1572868
  0.6 5.5 %copy-start.1 = (f32[1024,128]{1,0:T(8,128)S(1)}, f32[1024,128]{1,0:T(8,128)}, u32[]{:S(2)}) copy-start(f32[1024,128]{1,0:T(8,128)} %x_ref.5) | copy-start | bytes 1572868
  3.4 15.7 %collective-permute-start = (f32[512,128]{1,0:T(8,128)S(1)}, f32[512,128]{1,0:T(8,128)S(1)}, u32[]{:S(2)}, u32[]{:S(2)}) collective-permute-start(f32[512,128]{1,0:T(8,128)S(1)} %get-tuple-element.45), channel_id=1, source_target_pairs={{0,255},{1,2},{2,1},{3,4},{4,3},{5,6},{6,5},{7,8},{8,7},{9,10},{10... | collective-permute-start | bytes 786440 | tf_op jit(solution)/shard_map/ppermute | solution.py:455
  7.4 11.7 %collective-permute-start.1 = (f32[512,128]{1,0:T(8,128)S(1)}, f32[512,128]{1,0:T(8,128)S(1)}, u32[]{:S(2)}, u32[]{:S(2)}) collective-permute-start(f32[512,128]{1,0:T(8,128)S(1)} %get-tuple-element.46), channel_id=1, source_target_pairs={{0,1},{1,0},{2,3},{3,2},{4,5},{5,4},{6,7},{7,6},{8,9},{9,8},{10,11... | collective-permute-start | bytes 786440 | tf_op jit(solution)/shard_map/ppermute | solution.py:455
  19.1 5.5 %copy-start.2 = (f32[3,64,64]{2,1,0:T(8,128)S(1)}, f32[3,64,64]{2,1,0:T(8,128)}, u32[]{:S(2)}) copy-start(f32[3,64,64]{2,1,0:T(8,128)} %w_ref.7) | copy-start | bytes 147460
  20.7 1.3 %collective-permute-start.4 = (f32[56,128]{1,0:T(8,128)S(1)}, f32[56,128]{1,0:T(8,128)S(1)}, u32[]{:S(2)}, u32[]{:S(2)}) collective-permute-start(f32[56,128]{1,0:T(8,128)S(1)} %get-tuple-element.67), channel_id=1, source_target_pairs={{0,1},{1,0},{2,3},{3,2},{4,5},{5,4},{6,7},{7,6},{8,9},{9,8},{10,11... | collective-permute-start | bytes 86024 | tf_op jit(solution)/shard_map/ppermute | solution.py:455
  22.0 4.3 %collective-permute-start.7 = (f32[56,128]{1,0:T(8,128)S(1)}, f32[56,128]{1,0:T(8,128)S(1)}, u32[]{:S(2)}, u32[]{:S(2)}) collective-permute-start(f32[56,128]{1,0:T(8,128)S(1)} %add.24), channel_id=1, source_target_pairs={{0,4},{1,5},{2,6},{3,7},{4,0},{5,1},{6,2},{7,3},{8,12},{9,13},{10,... | collective-permute-start | bytes 86024 | tf_op jit(solution)/shard_map/ppermute | solution.py:455
  22.0 4.3 %collective-permute-start.6 = (f32[56,128]{1,0:T(8,128)S(1)}, f32[56,128]{1,0:T(8,128)S(1)}, u32[]{:S(2)}, u32[]{:S(2)}) collective-permute-start(f32[56,128]{1,0:T(8,128)S(1)} %add.24), channel_id=1, source_target_pairs={{0,6},{1,7},{2,4},{3,5},{4,2},{5,3},{6,0},{7,1},{8,14},{9,15},{10,... | collective-permute-start | bytes 86024 | tf_op jit(solution)/shard_map/ppermute | solution.py:455
  22.1 4.2 %collective-permute-start.5 = (f32[56,128]{1,0:T(8,128)S(1)}, f32[56,128]{1,0:T(8,128)S(1)}, u32[]{:S(2)}, u32[]{:S(2)}) collective-permute-start(f32[56,128]{1,0:T(8,128)S(1)} %add.24), channel_id=1, source_target_pairs={{0,2},{1,3},{2,0},{3,1},{4,6},{5,7},{6,4},{7,5},{8,10},{9,11},{10,... | collective-permute-start | bytes 86024 | tf_op jit(solution)/shard_map/ppermute | solution.py:455
  26.3 23.0 %copy-start.3 = (f32[64]{0:T(128)S(1)}, f32[64]{0:T(128)}, u32[]{:S(2)}) copy-start(f32[64]{0:T(128)} %param.10) | copy-start | bytes 772
  26.3 11.5 %collective-permute-start.10 = (f32[56,128]{1,0:T(8,128)S(1)}, f32[56,128]{1,0:T(8,128)S(1)}, u32[]{:S(2)}, u32[]{:S(2)}) collective-permute-start(f32[56,128]{1,0:T(8,128)S(1)} %add_add_fusion.1), channel_id=1, source_target_pairs={{0,128},{1,129},{2,130},{3,131},{4,132},{5,133},{6,134},{7,135},{8... | collective-permute-start | bytes 86024 | tf_op jit(solution)/shard_map/ppermute | solution.py:455
  26.9 10.9 %collective-permute-start.9 = (f32[56,128]{1,0:T(8,128)S(1)}, f32[56,128]{1,0:T(8,128)S(1)}, u32[]{:S(2)}, u32[]{:S(2)}) collective-permute-start(f32[56,128]{1,0:T(8,128)S(1)} %add_add_fusion.1), channel_id=1, source_target_pairs={{0,192},{1,193},{2,194},{3,195},{4,196},{5,197},{6,198},{7,199},{8... | collective-permute-start | bytes 86024 | tf_op jit(solution)/shard_map/ppermute | solution.py:455
  27.8 10.0 %collective-permute-start.8 = (f32[56,128]{1,0:T(8,128)S(1)}, f32[56,128]{1,0:T(8,128)S(1)}, u32[]{:S(2)}, u32[]{:S(2)}) collective-permute-start(f32[56,128]{1,0:T(8,128)S(1)} %add_add_fusion.1), channel_id=1, source_target_pairs={{0,64},{1,65},{2,66},{3,67},{4,68},{5,69},{6,70},{7,71},{8,72},{9,... | collective-permute-start | bytes 86024 | tf_op jit(solution)/shard_map/ppermute | solution.py:455
  30.7 21.7 %collective-permute-start.2 = (f32[512,128]{1,0:T(8,128)S(1)}, f32[512,128]{1,0:T(8,128)S(1)}, u32[]{:S(2)}, u32[]{:S(2)}) collective-permute-start(f32[512,128]{1,0:T(8,128)S(1)} %get-tuple-element.58), channel_id=1, source_target_pairs={{0,255},{1,2},{2,1},{3,4},{4,3},{5,6},{6,5},{7,8},{8,7},{9,10},{10... | collective-permute-start | bytes 786440 | tf_op jit(solution)/shard_map/ppermute | solution.py:455
  34.4 18.0 %collective-permute-start.3 = (f32[512,128]{1,0:T(8,128)S(1)}, f32[512,128]{1,0:T(8,128)S(1)}, u32[]{:S(2)}, u32[]{:S(2)}) collective-permute-start(f32[512,128]{1,0:T(8,128)S(1)} %get-tuple-element.59), channel_id=1, source_target_pairs={{0,1},{1,0},{2,3},{3,2},{4,5},{5,4},{6,7},{7,6},{8,9},{9,8},{10,11... | collective-permute-start | bytes 786440 | tf_op jit(solution)/shard_map/ppermute | solution.py:455
  37.8 3.3 %collective-permute-start.11 = (f32[56,128]{1,0:T(8,128)S(1)}, f32[56,128]{1,0:T(8,128)S(1)}, u32[]{:S(2)}, u32[]{:S(2)}) collective-permute-start(f32[56,128]{1,0:T(8,128)S(1)} %add_add_fusion), channel_id=1, source_target_pairs={{0,8},{1,9},{2,10},{3,11},{4,12},{5,13},{6,14},{7,15},{8,0},{9,1},... | collective-permute-start | bytes 86024 | tf_op jit(solution)/shard_map/ppermute | solution.py:455
  41.1 5.7 %collective-permute-start.14 = (f32[56,128]{1,0:T(8,128)S(1)}, f32[56,128]{1,0:T(8,128)S(1)}, u32[]{:S(2)}, u32[]{:S(2)}) collective-permute-start(f32[56,128]{1,0:T(8,128)S(1)} %add.31.own), channel_id=1, source_target_pairs={{0,40},{1,41},{2,42},{3,43},{4,44},{5,45},{6,46},{7,47},{8,32},{9,... | collective-permute-start | bytes 86024 | tf_op jit(solution)/shard_map/ppermute | solution.py:455
  41.1 5.7 %collective-permute-start.13 = (f32[56,128]{1,0:T(8,128)S(1)}, f32[56,128]{1,0:T(8,128)S(1)}, u32[]{:S(2)}, u32[]{:S(2)}) collective-permute-start(f32[56,128]{1,0:T(8,128)S(1)} %add.31.own), channel_id=1, source_target_pairs={{0,48},{1,49},{2,50},{3,51},{4,52},{5,53},{6,54},{7,55},{8,24},{9,... | collective-permute-start | bytes 86024 | tf_op jit(solution)/shard_map/ppermute | solution.py:455
  41.2 5.6 %collective-permute-start.12 = (f32[56,128]{1,0:T(8,128)S(1)}, f32[56,128]{1,0:T(8,128)S(1)}, u32[]{:S(2)}, u32[]{:S(2)}) collective-permute-start(f32[56,128]{1,0:T(8,128)S(1)} %add.31.own), channel_id=1, source_target_pairs={{0,56},{1,57},{2,58},{3,59},{4,60},{5,61},{6,62},{7,63},{8,16},{9,... | collective-permute-start | bytes 86024 | tf_op jit(solution)/shard_map/ppermute | solution.py:455
  46.9 4.7 %collective-permute-start.15 = (f32[56,128]{1,0:T(8,128)S(1)}, f32[56,128]{1,0:T(8,128)S(1)}, u32[]{:S(2)}, u32[]{:S(2)}) collective-permute-start(f32[56,128]{1,0:T(8,128)S(1)} %shard_map.101.mine), channel_id=1, source_target_pairs={{0,1},{1,0},{2,3},{3,2},{4,5},{5,4},{6,7},{7,6},{8,9},{9,8},{10,11... | collective-permute-start | bytes 86024 | tf_op jit(solution)/shard_map/ppermute | solution.py:455
